TPU v7x, 32 devices: a whole 2x2x4 slice. The times are simulated.
32 devices in a mesh: dp: 8 (over y, x, core), tensor: 4 (over z).
Axes of the slice: x: 2, y: 2, z: 4, core: 2. Of those that a mesh axis runs over, the one named last changes fastest.
Arguments:
- hidden_in: bfloat16 [16384, 1024], P(('dp', 'tensor')), may hold values from -6 to 6
- value_first: bfloat16 [16384, 1024], P('dp', 'tensor'), may hold values from -6 to 6
- segment_ids: int32 [16384], P('dp'), may hold values from 0 to 8, as said below
- gain_attn: float32 [1024], replicated, may hold values from 0.25 to 1.75
- w_query: bfloat16 [1024, 1024], P('dp', 'tensor'), may hold values from -0.1875 to 0.1875
- w_key: bfloat16 [1024, 1024], P('dp', 'tensor'), may hold values from -0.1875 to 0.1875
- w_value: bfloat16 [1024, 1024], P('dp', 'tensor'), may hold values from -0.1875 to 0.1875
- w_out: bfloat16 [1024, 1024], P('tensor', 'dp'), may hold values from -3 to 3
- gain_ffn: float32 [1024], replicated, may hold values from 0.25 to 1.75
- w_gate: bfloat16 [1024, 2816], P('dp', 'tensor'), may hold values from -0.1875 to 0.1875
- w_up: bfloat16 [1024, 2816], P('dp', 'tensor'), may hold values from -0.1875 to 0.1875
- w_down: bfloat16 [2816, 1024], P('tensor', 'dp'), may hold values from -0.109375 to 0.109375
- cotangent: bfloat16 [16384, 1024], P(('dp', 'tensor')), may hold values from -6 to 6
Outputs:
- output: bfloat16 [16384, 1024], P(('dp', 'tensor'))
- grad_input: float32 [16384, 1024], P(('dp', 'tensor'))
- grad_value_first: float32 [16384, 1024], P('dp', 'tensor')
- grad_gain_attn: float32 [1024], P(('dp', 'tensor'))
- grad_w_query: float32 [1024, 1024], P('dp', 'tensor')
- grad_w_key: float32 [1024, 1024], P('dp', 'tensor')
- grad_w_value: float32 [1024, 1024], P('dp', 'tensor')
- grad_w_out: float32 [1024, 1024], P('tensor', 'dp')
- grad_gain_ffn: float32 [1024], P(('dp', 'tensor'))
- grad_w_gate: float32 [1024, 2816], P('dp', 'tensor')
- grad_w_up: float32 [1024, 2816], P('dp', 'tensor')
- grad_w_down: float32 [2816, 1024], P('tensor', 'dp')
Inputs may be any that keep to these rules, and one draw needn't show every extreme that they name: `segment_ids`: in each group of 2048 tokens the first 1024 have id 0; then come continuations 1 to 8 in order, each of 64 to 192 tokens, and in every group one of them has exactly 192.
All inputs are finite; a program needn't handle non-finite values.
Results may differ from a plain program's by a relative error of at most 0.02.
Values may be sent and summed in bfloat16 or wider, within the bound.
No kernel may reach another device: no remote copies, remote signals or barrier semaphores. Data moves between devices by JAX's collectives and lax.ppermute only.
A program may use at most 192 MiB of HBM per device.

v0:
```python
import math

import jax
import jax.numpy as jnp
from jax import lax
from jax.sharding import PartitionSpec as P

HEAD_DIM = 64
PROMPT_LEN = 1024


epsilon = 1e-06


def block_rows(total_rows):
    block_size = min(512, total_rows)
    while total_rows % block_size:
        block_size = block_size + 1
    return block_size


def token_positions(segment):
    token_index = jnp.arange(segment.shape[0], dtype=jnp.int32)
    change = jnp.concatenate([jnp.ones((1,), dtype=jnp.bool_), segment[1:] != segment[:-1]])
    starts = lax.cummax(jnp.where(change, token_index, 0), axis=0)
    return token_index - starts + PROMPT_LEN * (segment > 0).astype(jnp.int32)


def rotation_tables(position):
    half_dim = HEAD_DIM // 2
    frequency = jnp.exp(
        jnp.arange(half_dim, dtype=jnp.float32) * (-2.0 * math.log(10000.0) / HEAD_DIM)
    )
    phase_angle = position.astype(jnp.float32)[:, None] * frequency[None, :]
    return (jnp.cos(phase_angle), jnp.sin(phase_angle))


def rotate(field, cosine, sine):
    row_count = field.shape[0]
    halves = field.reshape(row_count, -1, 2, HEAD_DIM // 2)
    first_half = halves[:, :, 0, :]
    second_half = halves[:, :, 1, :]
    cos_rows = cosine[:, None, :]
    sin_rows = sine[:, None, :]
    turned = jnp.stack(
        [
            first_half * cos_rows - second_half * sin_rows,
            second_half * cos_rows + first_half * sin_rows,
        ],
        axis=2,
    )
    return turned.reshape(row_count, -1)


def contract_rows(left, right):
    return lax.dot_general(
        left, right, (((0,), (0,)), ((), ())), preferred_element_type=jnp.float32
    )


def contract_cols(left, right):
    return lax.dot_general(
        left, right, (((1,), (1,)), ((), ())), preferred_element_type=jnp.float32
    )


def norm_rows(rows_in):
    inverse = lax.rsqrt(jnp.mean(rows_in * rows_in, axis=1, keepdims=True) + epsilon)
    return (rows_in * inverse, inverse)


def norm_back(grad_normed, scaled, inverse, gain_vector):
    weighted = grad_normed * gain_vector
    grad_rows = inverse * (weighted - scaled * jnp.mean(weighted * scaled, axis=1, keepdims=True))
    return (grad_rows, jnp.sum(grad_normed * scaled, axis=0))


def masked_scores(query_block, key_heads, segment_block, position_block, segment, position):
    query_heads = query_block.reshape(query_block.shape[0], -1, HEAD_DIM)
    scores = (
        jnp.einsum("qhd,khd->hqk", query_heads, key_heads, preferred_element_type=jnp.float32)
        * 0.125
    )
    visible = ((segment[None, :] == 0) | (segment[None, :] == segment_block[:, None])) & (
        position[None, :] <= position_block[:, None]
    )
    return (jnp.where(visible[None], scores, -1e30), query_heads)


def attention_forward(query_rot, key_rot, value_mix, segment, position):
    group_len, channels = query_rot.shape
    block_size = block_rows(group_len)
    block_count = group_len // block_size
    key_heads = key_rot.reshape(group_len, -1, HEAD_DIM)
    value_heads = value_mix.reshape(group_len, -1, HEAD_DIM)

    def one_block(block_inputs):
        query_block, segment_block, position_block = block_inputs
        scores, query_heads = masked_scores(
            query_block, key_heads, segment_block, position_block, segment, position
        )
        row_top = jnp.max(scores, axis=2, keepdims=True)
        expo = jnp.exp(scores - row_top)
        row_total = jnp.sum(expo, axis=2, keepdims=True)
        weights = (expo / row_total).astype(jnp.bfloat16)
        mixed_rows = jnp.einsum(
            "hqk,khd->qhd", weights, value_heads, preferred_element_type=jnp.float32
        )
        return (
            mixed_rows.reshape(block_size, channels).astype(jnp.bfloat16),
            row_top + jnp.log(row_total),
        )

    mixed_rows, log_totals = lax.map(
        one_block,
        (
            query_rot.reshape(block_count, block_size, channels),
            segment.reshape(block_count, block_size),
            position.reshape(block_count, block_size),
        ),
    )
    return (mixed_rows.reshape(group_len, channels), log_totals)


def attention_backward(query_rot, key_rot, value_mix, grad_attended, log_totals, segment, position):
    group_len, channels = query_rot.shape
    block_size = block_rows(group_len)
    block_count = group_len // block_size
    key_heads = key_rot.reshape(group_len, -1, HEAD_DIM)
    value_heads = value_mix.reshape(group_len, -1, HEAD_DIM)

    def one_block(running, block_inputs):
        grad_keys, grad_values = running
        query_block, grad_block, log_block, segment_block, position_block = block_inputs
        scores, query_heads = masked_scores(
            query_block, key_heads, segment_block, position_block, segment, position
        )
        probabilities = jnp.exp(scores - log_block)
        grad_heads = grad_block.reshape(block_size, -1, HEAD_DIM)
        grad_values = grad_values + jnp.einsum(
            "hqk,qhd->khd",
            probabilities.astype(jnp.bfloat16),
            grad_heads,
            preferred_element_type=jnp.float32,
        )
        grad_probs = jnp.einsum(
            "qhd,khd->hqk", grad_heads, value_heads, preferred_element_type=jnp.float32
        )
        row_delta = jnp.sum(probabilities * grad_probs, axis=2, keepdims=True)
        grad_scores = (probabilities * (grad_probs - row_delta)).astype(jnp.bfloat16)
        grad_query = (
            jnp.einsum("hqk,khd->qhd", grad_scores, key_heads, preferred_element_type=jnp.float32)
            * 0.125
        )
        grad_keys = (
            grad_keys
            + jnp.einsum(
                "hqk,qhd->khd", grad_scores, query_heads, preferred_element_type=jnp.float32
            )
            * 0.125
        )
        return ((grad_keys, grad_values), grad_query.reshape(block_size, channels))

    zero_carry = jnp.zeros((group_len, channels // HEAD_DIM, HEAD_DIM), jnp.float32)
    inputs = (
        query_rot.reshape(block_count, block_size, channels),
        grad_attended.reshape(block_count, block_size, channels),
        log_totals,
        segment.reshape(block_count, block_size),
        position.reshape(block_count, block_size),
    )
    (grad_keys, grad_values), grad_queries = lax.scan(one_block, (zero_carry, zero_carry), inputs)
    return (
        grad_queries.reshape(group_len, channels),
        grad_keys.reshape(group_len, channels),
        grad_values.reshape(group_len, channels),
    )


def on_device(
    hidden_in,
    value_first,
    segment_ids,
    gain_attn,
    w_query,
    w_key,
    w_value,
    w_out,
    gain_ffn,
    w_gate,
    w_up,
    w_down,
    cotangent,
):
    position = token_positions(segment_ids)
    cosine, sine = rotation_tables(position)
    forward_weights = (
        lax.all_gather(w_query, "dp", axis=0, tiled=True),
        lax.all_gather(w_key, "dp", axis=0, tiled=True),
        lax.all_gather(w_value, "dp", axis=0, tiled=True),
        lax.all_gather(w_out, "dp", axis=1, tiled=True),
        lax.all_gather(w_gate, "dp", axis=0, tiled=True),
        lax.all_gather(w_up, "dp", axis=0, tiled=True),
        lax.all_gather(w_down, "dp", axis=1, tiled=True),
    )
    query_full, key_full, value_full, out_full, gate_full, up_full, down_full = forward_weights
    hidden_rows = hidden_in.astype(jnp.float32)
    scaled_one, inverse_one = norm_rows(hidden_rows)
    normed_attn = (scaled_one * gain_attn).astype(jnp.bfloat16)
    normed_attn_all = lax.all_gather(normed_attn, "tensor", axis=0, tiled=True)
    query_rot = rotate(
        jnp.dot(normed_attn_all, query_full, preferred_element_type=jnp.float32), cosine, sine
    ).astype(jnp.bfloat16)
    key_rot = rotate(
        jnp.dot(normed_attn_all, key_full, preferred_element_type=jnp.float32), cosine, sine
    ).astype(jnp.bfloat16)
    value_mix = (
        0.5 * jnp.dot(normed_attn_all, value_full, preferred_element_type=jnp.float32)
        + 0.5 * value_first.astype(jnp.float32)
    ).astype(jnp.bfloat16)
    attended, log_totals = attention_forward(query_rot, key_rot, value_mix, segment_ids, position)
    middle = hidden_rows + lax.psum_scatter(
        jnp.dot(attended, out_full, preferred_element_type=jnp.float32).astype(jnp.bfloat16),
        "tensor",
        scatter_dimension=0,
        tiled=True,
    ).astype(jnp.float32)
    scaled_two, inverse_two = norm_rows(middle)
    normed_ffn = (scaled_two * gain_ffn).astype(jnp.bfloat16)
    normed_ffn_all = lax.all_gather(normed_ffn, "tensor", axis=0, tiled=True)
    gate_act = jnp.dot(normed_ffn_all, gate_full, preferred_element_type=jnp.float32)
    up_act = jnp.dot(normed_ffn_all, up_full, preferred_element_type=jnp.float32)
    sigmoid_gate = jax.nn.sigmoid(gate_act)
    silu_gate = gate_act * sigmoid_gate
    hidden_act = (silu_gate * up_act).astype(jnp.bfloat16)
    output = (
        middle
        + lax.psum_scatter(
            jnp.dot(hidden_act, down_full, preferred_element_type=jnp.float32).astype(jnp.bfloat16),
            "tensor",
            scatter_dimension=0,
            tiled=True,
        ).astype(jnp.float32)
    ).astype(jnp.bfloat16)
    backward_weights = (
        lax.all_gather(w_query, "dp", axis=0, tiled=True),
        lax.all_gather(w_key, "dp", axis=0, tiled=True),
        lax.all_gather(w_value, "dp", axis=0, tiled=True),
        lax.all_gather(w_out, "dp", axis=1, tiled=True),
        lax.all_gather(w_gate, "dp", axis=0, tiled=True),
        lax.all_gather(w_up, "dp", axis=0, tiled=True),
        lax.all_gather(w_down, "dp", axis=1, tiled=True),
    )
    query_back, key_back, value_back, out_back, gate_back, up_back, down_back = backward_weights
    cotangent_all = lax.all_gather(cotangent, "tensor", axis=0, tiled=True)
    grad_hidden = contract_cols(cotangent_all, down_back)
    grad_down_cols = contract_rows(cotangent_all, hidden_act)
    grad_gate = (
        grad_hidden * up_act * sigmoid_gate * (1.0 + gate_act * (1.0 - sigmoid_gate))
    ).astype(jnp.bfloat16)
    grad_up = (grad_hidden * silu_gate).astype(jnp.bfloat16)
    grad_gate_w = contract_rows(normed_ffn_all, grad_gate)
    grad_up_w = contract_rows(normed_ffn_all, grad_up)
    grad_normed_ffn = lax.psum_scatter(
        (contract_cols(grad_gate, gate_back) + contract_cols(grad_up, up_back)).astype(
            jnp.bfloat16
        ),
        "tensor",
        scatter_dimension=0,
        tiled=True,
    ).astype(jnp.float32)
    grad_rows_two, gain_two_part = norm_back(grad_normed_ffn, scaled_two, inverse_two, gain_ffn)
    grad_middle = cotangent.astype(jnp.float32) + grad_rows_two
    grad_middle_all = lax.all_gather(grad_middle.astype(jnp.bfloat16), "tensor", axis=0, tiled=True)
    grad_attended = contract_cols(grad_middle_all, out_back).astype(jnp.bfloat16)
    grad_out_cols = contract_rows(grad_middle_all, attended)
    grad_query, grad_key, grad_value = attention_backward(
        query_rot, key_rot, value_mix, grad_attended, log_totals, segment_ids, position
    )
    grad_query_proj = rotate(grad_query, cosine, -sine).astype(jnp.bfloat16)
    grad_key_proj = rotate(grad_key, cosine, -sine).astype(jnp.bfloat16)
    grad_value_proj = (0.5 * grad_value).astype(jnp.bfloat16)
    grad_value_first = 0.5 * grad_value
    grad_query_w = contract_rows(normed_attn_all, grad_query_proj)
    grad_key_w = contract_rows(normed_attn_all, grad_key_proj)
    grad_value_w = contract_rows(normed_attn_all, grad_value_proj)
    query_sum, key_sum, value_sum, out_sum, gate_sum, up_sum, down_sum = (
        lax.psum_scatter(grad_query_w, "dp", scatter_dimension=0, tiled=True),
        lax.psum_scatter(grad_key_w, "dp", scatter_dimension=0, tiled=True),
        lax.psum_scatter(grad_value_w, "dp", scatter_dimension=0, tiled=True),
        lax.psum_scatter(grad_out_cols, "dp", scatter_dimension=0, tiled=True),
        lax.psum_scatter(grad_gate_w, "dp", scatter_dimension=0, tiled=True),
        lax.psum_scatter(grad_up_w, "dp", scatter_dimension=0, tiled=True),
        lax.psum_scatter(grad_down_cols, "dp", scatter_dimension=0, tiled=True),
    )
    grad_normed_attn = lax.psum_scatter(
        (
            contract_cols(grad_query_proj, query_back)
            + contract_cols(grad_key_proj, key_back)
            + contract_cols(grad_value_proj, value_back)
        ).astype(jnp.bfloat16),
        "tensor",
        scatter_dimension=0,
        tiled=True,
    ).astype(jnp.float32)
    grad_rows_one, gain_one_part = norm_back(grad_normed_attn, scaled_one, inverse_one, gain_attn)
    grad_input = grad_middle + grad_rows_one
    gain_one_sum, gain_two_sum = (
        lax.psum_scatter(gain_one_part, ("dp", "tensor"), scatter_dimension=0, tiled=True),
        lax.psum_scatter(gain_two_part, ("dp", "tensor"), scatter_dimension=0, tiled=True),
    )
    return (
        output,
        grad_input,
        grad_value_first,
        gain_one_sum,
        query_sum,
        key_sum,
        value_sum,
        out_sum.T,
        gain_two_sum,
        gate_sum,
        up_sum,
        down_sum.T,
    )


def solution(mesh):
    return jax.shard_map(
        on_device,
        mesh=mesh,
        in_specs=(
            P(("dp", "tensor"), None),
            P("dp", "tensor"),
            P("dp"),
            P(),
            P("dp", "tensor"),
            P("dp", "tensor"),
            P("dp", "tensor"),
            P("tensor", "dp"),
            P(),
            P("dp", "tensor"),
            P("dp", "tensor"),
            P("tensor", "dp"),
            P(("dp", "tensor"), None),
        ),
        out_specs=(
            P(("dp", "tensor"), None),
            P(("dp", "tensor"), None),
            P("dp", "tensor"),
            P(("dp", "tensor")),
            P("dp", "tensor"),
            P("dp", "tensor"),
            P("dp", "tensor"),
            P("tensor", "dp"),
            P(("dp", "tensor")),
            P("dp", "tensor"),
            P("dp", "tensor"),
            P("tensor", "dp"),
        ),
        check_vma=False,
    )
```

profile of v0, /device:TPU:0, one launch (start us, length us, event | category | flops | bytes accessed | tf_op | source)
XLA Modules:
  0.0 1384.2 jit_solution(16359954803292189402)
XLA Ops:
  15.8 11.3 all_gather.41
  59.5 36.4 %all-gather.8.cloned.1.call-done = bf16[2048,1024]{1,0:T(8,128)(2,1)} async-done(((bf16[512,1024]{1,0:T(8,128)(2,1)}), bf16[2048,1024]{1,0:T(8,128)(2,1)}) %all-gather.8.cloned.1.call-update) | async-done | bytes 4194320 | tf_op jit(solution)/shard_map/all_gather | solution.py:210
  109.4 67.3 %while.27 = (s32[]{:T(128)}, bf16[4,512,256]{2,1,0:T(8,128)(2,1)}, f32[4,4,512,1]{2,1,3,0:T(4,128)}, s32[2048]{0:T(1024)S(1)}, s32[4,512]{1,0:T(4,128)}, /*index...) while((s32[]{:T(128)}, bf16[4,512,256]{2,1,0:T(8,128)(2,1)}, ...), condition=%wide.region_6.7_spmd, body=%wide.region_3.6_spmd.sunk | while | flops 1128398848 | bytes 58826884 | solution.py:114
  182.9 74.8 %reduce-scatter.12.cloned.1.call-done = bf16[512,1024]{1,0:T(8,128)(2,1)} async-done(((bf16[2048,1024]{1,0:T(8,128)(2,1)}), bf16[512,1024]{1,0:T(8,128)(2,1)}) %reduce-scatter.12.cloned.1.call-update) | async-done | bytes 1048592 | tf_op jit(solution)/shard_map/reduce_scatter | solution.py:222
  264.1 79.1 %all-gather.10.cloned.1.call-done = bf16[2048,1024]{1,0:T(8,128)(2,1)} async-done(((bf16[512,1024]{1,0:T(8,128)(2,1)}), bf16[2048,1024]{1,0:T(8,128)(2,1)}) %all-gather.10.cloned.1.call-update) | async-done | bytes 4194320 | tf_op jit(solution)/shard_map/all_gather | solution.py:230
  351.5 17.3 %all-gather.12.cloned.1.call-done = bf16[1024,704]{0,1:T(8,128)(2,1)} async-done(((bf16[128,704]{0,1:T(8,128)(2,1)}), bf16[1024,704]{0,1:T(8,128)(2,1)}) %all-gather.12.cloned.1.call-update) | async-done | bytes 1441808 | tf_op jit(solution)/shard_map/all_gather | solution.py:202
  377.1 18.9 %all-gather.16.cloned.1.call-done = bf16[704,1024]{1,0:T(8,128)(2,1)} async-done(((bf16[704,128]{1,0:T(8,128)(2,1)}), bf16[704,1024]{1,0:T(8,128)(2,1)}) %all-gather.16.cloned.1.call-update) | async-done | bytes 1441808 | tf_op jit(solution)/shard_map/all_gather | solution.py:204
  396.0 82.3 %all-gather.18.cloned.1.call-done = bf16[2048,1024]{1,0:T(8,128)(2,1)} async-done(((bf16[512,1024]{1,0:T(8,128)(2,1)}), bf16[2048,1024]{1,0:T(8,128)(2,1)}) %all-gather.18.cloned.1.call-update) | async-done | bytes 4194320 | tf_op jit(solution)/shard_map/all_gather | solution.py:255
  478.3 12.1 multiply_convert_fusion.1
  499.1 75.4 %reduce-scatter.16.cloned.1.call-done = bf16[512,1024]{1,0:T(8,128)(2,1)} async-done(((bf16[2048,1024]{1,0:T(8,128)(2,1)}), bf16[512,1024]{1,0:T(8,128)(2,1)}) %reduce-scatter.16.cloned.1.call-update) | async-done | bytes 1048592 | tf_op jit(solution)/shard_map/reduce_scatter | solution.py:264
  579.4 81.1 %all-gather.20.cloned.1.call-done = bf16[2048,1024]{1,0:T(8,128)(2,1)} async-done(((bf16[512,1024]{1,0:T(8,128)(2,1)}), bf16[2048,1024]{1,0:T(8,128)(2,1)}) %all-gather.20.cloned.1.call-update) | async-done | bytes 4194320 | tf_op jit(solution)/shard_map/all_gather | solution.py:274
  665.2 242.0 %while.28 = (s32[]{:T(128)}, f32[2048,4,64]{0,2,1:T(8,128)}, f32[2048,4,64]{0,2,1:T(8,128)}, f32[4,512,256]{1,0,2:T(4,128)}, bf16[4,512,256]{1,2,0:T(8,128)(2,1)...) while((s32[]{:T(128)}, f32[2048,4,64]{0,2,1:T(8,128)}, ...), condition=%wide.region_14.15_spmd.clone, body=%wide.region_12.14_spmd.clone.sunk | while | flops 2754215936 | bytes 187892144 | solution.py:172
  680.2 11.6 multiply_reduce_fusion.3
  691.9 11.0 multiply_convert_fusion.6
  712.6 11.0 dynamic_update_slice.20
  739.7 11.6 multiply_reduce_fusion.3
  751.3 11.0 multiply_convert_fusion.6
  773.7 11.0 dynamic_update_slice.20
  800.7 11.6 multiply_reduce_fusion.3
  812.4 11.0 multiply_convert_fusion.6
  834.7 11.0 dynamic_update_slice.20
  861.8 11.6 multiply_reduce_fusion.3
  895.7 11.0 dynamic_update_slice.20
  977.4 51.8 %reduce-scatter.18.cloned.1.call-done = bf16[512,1024]{1,0:T(8,128)(2,1)} async-done(((bf16[2048,1024]{1,0:T(8,128)(2,1)}), bf16[512,1024]{1,0:T(8,128)(2,1)}) %reduce-scatter.18.cloned.1.call-update) | async-done | bytes 1048592 | tf_op jit(solution)/shard_map/reduce_scatter | solution.py:296
  1031.2 42.9 %all-reduce.2 = (f32[1024]{0:T(1024)S(1)}, f32[1024]{0:T(1024)S(1)}) all-reduce(f32[1024]{0:T(1024)S(1)} %get-tuple-element.278, f32[1024]{0:T(1024)S(1)} %copy-done.49), channel_id=6, replica_groups=mesh['dp'=8,'tensor'=4] {'dp','tensor'}, use_global_device_ids=true, to_apply=%region_18.19.clone | all-reduce | flops 2048 | bytes 16384
  1075.2 34.3 %reduce-scatter.14.cloned.1.call-done = bf16[512,1024]{1,0:T(8,128)(2,1)} async-done(((bf16[2048,1024]{1,0:T(8,128)(2,1)}), bf16[512,1024]{1,0:T(8,128)(2,1)}) %reduce-scatter.14.cloned.1.call-update) | async-done | bytes 1048592 | tf_op jit(solution)/shard_map/reduce_scatter | solution.py:238
  1113.9 44.9 %reduce-scatter.32.cloned.1.call-done = f32[128,704]{0,1:T(8,128)} async-done(((f32[1024,704]{0,1:T(8,128)}), f32[128,704]{0,1:T(8,128)}) %reduce-scatter.32.cloned.1.call-update) | async-done | bytes 360464 | tf_op jit(solution)/shard_map/reduce_scatter | solution.py:294
  1158.8 49.0 %reduce-scatter.28.cloned.1.call-done = f32[128,704]{0,1:T(8,128)} async-done(((f32[1024,704]{0,1:T(8,128)}), f32[128,704]{0,1:T(8,128)}) %reduce-scatter.28.cloned.1.call-update) | async-done | bytes 360464 | tf_op jit(solution)/shard_map/reduce_scatter | solution.py:292
  1207.8 48.8 %reduce-scatter.30.cloned.1.call-done = f32[128,704]{0,1:T(8,128)} async-done(((f32[1024,704]{0,1:T(8,128)}), f32[128,704]{0,1:T(8,128)}) %reduce-scatter.30.cloned.1.call-update) | async-done | bytes 360464 | tf_op jit(solution)/shard_map/reduce_scatter | solution.py:293
  1256.6 39.9 %reduce-scatter.22.cloned.1.call-done = f32[128,256]{1,0:T(8,128)} async-done(((f32[1024,256]{1,0:T(8,128)}), f32[128,256]{1,0:T(8,128)}) %reduce-scatter.22.cloned.1.call-update) | async-done | bytes 131088 | tf_op jit(solution)/shard_map/reduce_scatter | solution.py:289
  1296.5 40.1 %reduce-scatter.20.cloned.1.call-done = f32[128,256]{1,0:T(8,128)} async-done(((f32[1024,256]{1,0:T(8,128)}), f32[128,256]{1,0:T(8,128)}) %reduce-scatter.20.cloned.1.call-update) | async-done | bytes 131088 | tf_op jit(solution)/shard_map/reduce_scatter | solution.py:288
  1336.6 40.1 %reduce-scatter.24.cloned.1.call-done = f32[128,256]{1,0:T(8,128)} async-done(((f32[1024,256]{1,0:T(8,128)}), f32[128,256]{1,0:T(8,128)}) %reduce-scatter.24.cloned.1.call-update) | async-done | bytes 131088 | tf_op jit(solution)/shard_map/reduce_scatter | solution.py:290
  (350 shorter events, 362.0 us)
Async XLA Ops:
  8.0 87.9 %all-gather.8.cloned.1.call-start = ((), (), s32[]{:S(2)}) async-start(), calls=%async_computation.11 | async-start | bytes 5242880 | tf_op jit(solution)/shard_map/all_gather | solution.py:210
  12.3 245.4 %reduce-scatter.12.cloned.1.call-start = ((), (), s32[]{:S(2)}) async-start(), calls=%async_computation.12 | async-start | bytes 5242880 | tf_op jit(solution)/shard_map/reduce_scatter | solution.py:222
  27.1 72.5 %copy-start.24 = (bf16[1024,256]{1,0:T(8,128)(2,1)}, bf16[1024,256]{1,0:T(8,128)(2,1)S(1)}, u32[]{:S(2)}) copy-start(bf16[1024,256]{1,0:T(8,128)(2,1)S(1)} %all_gather.41) | copy-start | bytes 1572868
  36.9 62.7 %copy-start.22 = (bf16[1024,256]{1,0:T(8,128)(2,1)}, bf16[1024,256]{1,0:T(8,128)(2,1)S(1)}, u32[]{:S(2)}) copy-start(bf16[1024,256]{1,0:T(8,128)(2,1)S(1)} %all_gather.42) | copy-start | bytes 1572868
  109.4 68.3 %copy-start.26 = (bf16[256,1024]{1,0:T(8,128)(2,1)S(1)}, bf16[256,1024]{1,0:T(8,128)(2,1)}, u32[]{:S(2)}) copy-start(bf16[256,1024]{1,0:T(8,128)(2,1)} %all_gather.44) | copy-start | bytes 1572868
  182.2 75.5 %copy-start.3 = (bf16[512,1024]{1,0:T(8,128)(2,1)S(1)}, bf16[512,1024]{1,0:T(8,128)(2,1)}, u32[]{:S(2)}) copy-start(bf16[512,1024]{1,0:T(8,128)(2,1)} %param.17) | copy-start | bytes 3145732
  182.2 77.1 %copy-start.36 = (f32[1024]{0:T(1024)S(1)}, f32[1024]{0:T(1024)}, u32[]{:S(2)}) copy-start(f32[1024]{0:T(1024)} %param.25) | copy-start | bytes 12292
  182.2 81.9 %all-gather.14.cloned.1.call-start = ((), (), s32[]{:S(2)}) async-start(), calls=%async_computation.15 | async-start | bytes 1622016 | tf_op jit(solution)/shard_map/all_gather | solution.py:203
  182.8 160.4 %all-gather.10.cloned.1.call-start = ((), (), s32[]{:S(2)}) async-start(), calls=%async_computation.13 | async-start | bytes 5242880 | tf_op jit(solution)/shard_map/all_gather | solution.py:230
  259.3 318.0 %copy-start.42 = (f32[512]{0:T(512)}, f32[512]{0:T(512)S(1)}, u32[]{:S(2)}) copy-start(f32[512]{0:T(512)S(1)} %add_rsqrt_fusion) | copy-start | bytes 6148
  262.0 106.8 %all-gather.12.cloned.1.call-start = ((), (), s32[]{:S(2)}) async-start(), calls=%async_computation.14 | async-start | bytes 1622016 | tf_op jit(solution)/shard_map/all_gather | solution.py:202
  262.5 133.4 %all-gather.16.cloned.1.call-start = ((), (), s32[]{:S(2)}) async-start(), calls=%async_computation.16 | async-start | bytes 1622016 | tf_op jit(solution)/shard_map/all_gather | solution.py:204
  263.3 215.0 %all-gather.18.cloned.1.call-start = ((), (), s32[]{:S(2)}) async-start(), calls=%async_computation.18 | async-start | bytes 5242880 | tf_op jit(solution)/shard_map/all_gather | solution.py:255
  264.0 310.5 %reduce-scatter.16.cloned.1.call-start = ((), (), s32[]{:S(2)}) async-start(), calls=%async_computation.19 | async-start | bytes 5242880 | tf_op jit(solution)/shard_map/reduce_scatter | solution.py:264
  499.1 75.5 %copy-start.9 = (bf16[512,1024]{1,0:T(8,128)(2,1)S(1)}, bf16[512,1024]{1,0:T(8,128)(2,1)}, u32[]{:S(2)}) copy-start(bf16[512,1024]{1,0:T(8,128)(2,1)} %reduce-scatter.12.cloned.1.call-done) | copy-start | bytes 3145732
  499.1 161.5 %all-gather.20.cloned.1.call-start = ((), (), s32[]{:S(2)}) async-start(), calls=%async_computation.20 | async-start | bytes 5242880 | tf_op jit(solution)/shard_map/all_gather | solution.py:274
  579.3 396.4 %reduce-scatter.26.cloned.1.call-start = ((), (), s32[]{:S(2)}) async-start(), calls=%async_computation.25 | async-start | bytes 1179648 | tf_op jit(solution)/shard_map/reduce_scatter | solution.py:291
  915.6 113.6 %reduce-scatter.18.cloned.1.call-start = ((), (), s32[]{:S(2)}) async-start(), calls=%async_computation.21 | async-start | bytes 5242880 | tf_op jit(solution)/shard_map/reduce_scatter | solution.py:296
  926.2 183.4 %reduce-scatter.14.cloned.1.call-start = ((), (), s32[]{:S(2)}) async-start(), calls=%async_computation.17 | async-start | bytes 5242880 | tf_op jit(solution)/shard_map/reduce_scatter | solution.py:238
  934.0 224.8 %reduce-scatter.32.cloned.1.call-start = ((), (), s32[]{:S(2)}) async-start(), calls=%async_computation.28 | async-start | bytes 3244032 | tf_op jit(solution)/shard_map/reduce_scatter | solution.py:294
  942.0 265.8 %reduce-scatter.28.cloned.1.call-start = ((), (), s32[]{:S(2)}) async-start(), calls=%async_computation.26 | async-start | bytes 3244032 | tf_op jit(solution)/shard_map/reduce_scatter | solution.py:292
  949.9 306.7 %reduce-scatter.30.cloned.1.call-start = ((), (), s32[]{:S(2)}) async-start(), calls=%async_computation.27 | async-start | bytes 3244032 | tf_op jit(solution)/shard_map/reduce_scatter | solution.py:293
  957.8 338.7 %reduce-scatter.22.cloned.1.call-start = ((), (), s32[]{:S(2)}) async-start(), calls=%async_computation.23 | async-start | bytes 1179648 | tf_op jit(solution)/shard_map/reduce_scatter | solution.py:289
  963.2 373.4 %reduce-scatter.20.cloned.1.call-start = ((), (), s32[]{:S(2)}) async-start(), calls=%async_computation.22 | async-start | bytes 1179648 | tf_op jit(solution)/shard_map/reduce_scatter | solution.py:288
  967.8 408.9 %reduce-scatter.24.cloned.1.call-start = ((), (), s32[]{:S(2)}) async-start(), calls=%async_computation.24 | async-start | bytes 1179648 | tf_op jit(solution)/shard_map/reduce_scatter | solution.py:290
  972.5 56.6 %copy-start.46 = (f32[512]{0:T(512)S(1)}, f32[512]{0:T(512)}, u32[]{:S(2)}) copy-start(f32[512]{0:T(512)} %copy-done.45) | copy-start | bytes 6148
  972.6 58.6 %copy-start.49 = (f32[1024]{0:T(1024)S(1)}, f32[1024]{0:T(1024)}, u32[]{:S(2)}) copy-start(f32[1024]{0:T(1024)} %get-tuple-element.276) | copy-start | bytes 12292
  972.6 137.0 %copy-start.10 = (bf16[512,1024]{1,0:T(8,128)(2,1)S(1)}, bf16[512,1024]{1,0:T(8,128)(2,1)}, u32[]{:S(2)}) copy-start(bf16[512,1024]{1,0:T(8,128)(2,1)} %reduce-scatter.12.cloned.1.call-done) | copy-start | bytes 3145732
  972.6 137.0 %copy-start.13 = (bf16[512,1024]{1,0:T(8,128)(2,1)S(1)}, bf16[512,1024]{1,0:T(8,128)(2,1)}, u32[]{:S(2)}) copy-start(bf16[512,1024]{1,0:T(8,128)(2,1)} %param.29) | copy-start | bytes 3145732
  972.6 137.0 %copy-start.37 = (f32[1024]{0:T(1024)S(1)}, f32[1024]{0:T(1024)}, u32[]{:S(2)}) copy-start(f32[1024]{0:T(1024)} %param.25) | copy-start | bytes 12292
  972.6 137.0 %copy-start.43 = (f32[512]{0:T(512)S(1)}, f32[512]{0:T(512)}, u32[]{:S(2)}) copy-start(f32[512]{0:T(512)} %copy-done.42) | copy-start | bytes 6148
  972.6 137.0 %copy-start.48 = (f32[512]{0:T(512)S(1)}, f32[512]{0:T(512)}, u32[]{:S(2)}) copy-start(f32[512]{0:T(512)} %copy-done.47) | copy-start | bytes 6148
  (65 other events, 585.2 us)
Sparse Core Ops, SparseCore 0:
  12.4 83.4 all-gather.7
  182.4 75.2 reduce-scatter.11
  499.2 75.2 reduce-scatter.15
Sparse Core Ops, SparseCore 1:
  184.6 23.6 all-gather.13
  262.0 81.1 all-gather.9
  345.1 23.6 all-gather.11
  370.8 25.1 all-gather.15
  397.6 80.6 all-gather.17
  579.4 81.1 all-gather.19
  915.6 34.5 reduce-scatter.25
  952.3 76.7 reduce-scatter.17
  1031.4 78.1 reduce-scatter.13
  1113.5 45.2 reduce-scatter.31
  1163.0 44.7 reduce-scatter.27
  1211.8 44.8 reduce-scatter.29
  1260.5 35.9 reduce-scatter.21
  1300.6 35.9 reduce-scatter.19
  1340.7 35.9 reduce-scatter.23
where the time goes:
time: 1400 us; the launch traced here: 1380 us
  waiting for transfers between devices  817 us (58%)
  matrix products  269 us (19%)
  other arithmetic  101 us (7%)
  local copies, waits for them, and re-layouts  93.2 us (7%)
  blocking collectives  84.8 us (6%)
  between operations  16.4 us (1%)
    all_gather x1, waiting for transfers between devices, on_device(): cotangent_all = lax.all_gather(cotangent, 'tensor', axis=0, tiled=True)  82.3 us
    all_gather x1, waiting for transfers between devices, on_device(): lax.all_gather(grad_middle.astype(jnp.bfloat16), 'tensor', axis=0, tiled=...  81.1 us
    all_gather x1, waiting for transfers between devices, on_device(): normed_ffn_all = lax.all_gather(normed_ffn, 'tensor', axis=0, tiled=True)  79.1 us
    reduce_scatter x1, waiting for transfers between devices, on_device(): lax.psum_scatter((contract_cols(grad_gate, gate_back) + contract_cols(gra...  75.4 us
    reduce_scatter x1, waiting for transfers between devices, on_device(): lax.psum_scatter(jnp.dot(attended, out_full, preferred_element_type=jnp.f...  74.8 us
    reduce_scatter x1, waiting for transfers between devices, on_device(): lax.psum_scatter((contract_cols(grad_query_proj, query_back) + contract_c...  51.8 us
    reduce_scatter x1, waiting for transfers between devices, on_device(): lax.psum_scatter(grad_gate_w, 'dp', scatter_dimension=0, tiled=True)  49 us
    reduce_scatter x1, waiting for transfers between devices, on_device(): lax.psum_scatter(grad_up_w, 'dp', scatter_dimension=0, tiled=True)  48.8 us
  transfers between devices with their start and end apart: 18, of which 16 were waited for; matrix products, arithmetic and copies ran while one was open for 7% of the time, Pallas kernels for 0%

commit v1 on v0

v1 whole, which is shorter than its diff:
```python
import functools
import math

import jax
import jax.numpy as jnp
from jax import lax
from jax.experimental import pallas as pl
from jax.experimental.pallas import tpu as pltpu
from jax.sharding import Mesh
from jax.sharding import PartitionSpec as P

HEAD_DIM = 64
PROMPT_LEN = 1024
BLOCK = 256
BF16 = jnp.bfloat16
F32 = jnp.float32
VMEM_LIMIT = 56 * 1024 * 1024

epsilon = 1e-06


def token_positions(segment):
    ids = jnp.arange(1, 9, dtype=jnp.int32)
    token_index = jnp.arange(segment.shape[0], dtype=jnp.int32)
    starts = jnp.sum((segment[None, :] < ids[:, None]).astype(jnp.int32), axis=1)
    own = jnp.sum(jnp.where(segment[None, :] == ids[:, None], starts[:, None], 0), axis=0)
    return token_index - own + PROMPT_LEN * (segment > 0).astype(jnp.int32)


def rotation_tables(position):
    half_dim = HEAD_DIM // 2
    frequency = jnp.exp(
        jnp.arange(half_dim, dtype=F32) * (-2.0 * math.log(10000.0) / HEAD_DIM)
    )
    angle = position.astype(F32)[:, None] * frequency[None, :]
    cosine, sine = jnp.cos(angle), jnp.sin(angle)
    return (
        jnp.concatenate([cosine] * 4, axis=1),
        jnp.concatenate([-sine, sine] * 2, axis=1),
    )


def contract_rows(left, right):
    return lax.dot_general(left, right, (((0,), (0,)), ((), ())), preferred_element_type=F32)


def contract_cols(left, right):
    return lax.dot_general(left, right, (((1,), (1,)), ((), ())), preferred_element_type=F32)


def matmul(left, right):
    return jnp.dot(left, right, preferred_element_type=F32)


def turn(field, cosine, sine):
    lane = lax.broadcasted_iota(jnp.int32, cosine.shape, 1)
    first = (lane % HEAD_DIM) < HEAD_DIM // 2
    parts = []
    for start in range(0, field.shape[1], 128):
        part = field[:, start : start + 128]
        partner = jnp.where(first, pltpu.roll(part, 96, 1), pltpu.roll(part, 32, 1))
        parts.append(part * cosine + partner * sine)
    return jnp.concatenate(parts, axis=1)


def project_kernel(
    blk_ref, x_ref, w_ref, gain_ref, cos_ref, sin_ref, first_ref, *rest
):
    n_ref, q_ref, k_ref, v_ref = rest[-4:]
    x = x_ref[...].astype(F32)
    inverse = lax.rsqrt(jnp.mean(x * x, axis=1, keepdims=True) + epsilon)
    normed = (x * inverse * gain_ref[...]).astype(BF16)
    n_ref[...] = normed
    width = q_ref.shape[1]
    cosine, sine = cos_ref[...], sin_ref[...]
    q_ref[...] = turn(matmul(normed, w_ref[:, :width]), cosine, sine).astype(BF16)
    k_ref[...] = turn(matmul(normed, w_ref[:, width : 2 * width]), cosine, sine).astype(BF16)
    v_ref[...] = (
        0.5 * matmul(normed, w_ref[:, 2 * width :]) + 0.5 * first_ref[...].astype(F32)
    ).astype(BF16)


def project(block, before, x_part, w_qkv, gain, cosine, sine, value_first):
    rows, model = x_part.shape
    tokens, width = value_first.shape
    row = lambda cols: pl.BlockSpec((rows, cols), lambda i, b: (b[0], 0))
    whole = lambda shape: pl.BlockSpec(shape, lambda i, b: (0, 0))
    return pl.pallas_call(
        project_kernel,
        grid_spec=pltpu.PrefetchScalarGridSpec(
            num_scalar_prefetch=1,
            grid=(1,),
            in_specs=[
                whole((rows, model)), whole(w_qkv.shape), whole((1, model)),
                row(128), row(128), row(width),
            ] + [pl.BlockSpec(memory_space=pl.ANY)] * len(before),
            out_specs=[row(model), row(width), row(width), row(width)],
        ),
        out_shape=[jax.ShapeDtypeStruct((tokens, model), BF16)]
        + [jax.ShapeDtypeStruct((tokens, width), BF16)] * 3,
        input_output_aliases={7 + i: i for i in range(len(before))},
        compiler_params=pltpu.CompilerParams(vmem_limit_bytes=VMEM_LIMIT),
        cost_estimate=pl.CostEstimate(
            flops=2 * rows * model * 3 * width, bytes_accessed=5 << 20, transcendentals=0
        ),
        name="project",
    )(block, x_part, w_qkv, gain, cosine, sine, value_first, *before)


def unproject_kernel(final, blk_ref, g_ref, w_ref, x_ref, gain_ref, *rest):
    part = contract_cols(g_ref[...], w_ref[...])
    x = x_ref[...].astype(F32)
    inverse = lax.rsqrt(jnp.mean(x * x, axis=1, keepdims=True) + epsilon)
    scaled = x * inverse
    rest[-1][...] = jnp.sum(part * scaled, axis=0, keepdims=True)
    if len(rest) > 2:
        part = part + rest[0][...].astype(F32)
    if not final:
        rest[-2][...] = part.astype(BF16)
        return
    weighted = part * gain_ref[...]
    rest[-2][...] = rest[1][...] + inverse * (
        weighted - scaled * jnp.mean(weighted * scaled, axis=1, keepdims=True)
    )


def unproject(block, qkv_grads, w_qkv, x_part, gain, arrived, grad_middle):
    rows, model = x_part.shape
    final = grad_middle is not None
    whole = lambda shape: pl.BlockSpec(shape, lambda i, b: (0, 0))
    more = [v for v in (arrived, grad_middle) if v is not None]
    return pl.pallas_call(
        functools.partial(unproject_kernel, final),
        grid_spec=pltpu.PrefetchScalarGridSpec(
            num_scalar_prefetch=1,
            grid=(1,),
            in_specs=[
                pl.BlockSpec((rows, qkv_grads.shape[1]), lambda i, b: (b[0], 0)),
                whole(w_qkv.shape), whole((rows, model)), whole((1, model)),
            ] + [whole((rows, model))] * len(more),
            out_specs=[whole((rows, model)), whole((1, model))],
        ),
        out_shape=[
            jax.ShapeDtypeStruct((rows, model), F32 if final else BF16),
            jax.ShapeDtypeStruct((1, model), F32),
        ],
        compiler_params=pltpu.CompilerParams(vmem_limit_bytes=VMEM_LIMIT),
        cost_estimate=pl.CostEstimate(
            flops=2 * rows * model * qkv_grads.shape[1], bytes_accessed=5 << 20, transcendentals=0
        ),
        name="unproject",
    )(block, qkv_grads, w_qkv, x_part, gain, *more)


def head_lanes(width, head):
    lane = lax.broadcasted_iota(jnp.int32, (1, width), 1)
    return (lane // HEAD_DIM) == head


def attend_kernel(q_ref, k_ref, v_ref, segc_ref, segr_ref, o_ref, lse_ref, qh_ref, acc_ref):
    head = pl.program_id(0)
    tokens, width = q_ref.shape
    keep = head_lanes(width, head)
    keep_low = jnp.where(keep, 0.125, 0.0).astype(BF16)
    qh_ref[...] = q_ref[...] * keep_low
    prompt_blocks = PROMPT_LEN // BLOCK

    @pl.when(head == 0)
    def _():
        acc_ref[...] = jnp.zeros_like(acc_ref)

    for qi in range(tokens // BLOCK):
        q0 = qi * BLOCK
        query = qh_ref[q0 : q0 + BLOCK, :]
        plain = qi if qi < prompt_blocks else prompt_blocks
        first_masked = qi if qi <= prompt_blocks else qi - 1
        row_ids = q0 + lax.broadcasted_iota(jnp.int32, (BLOCK, 1), 0)
        scores, tops = [], []
        if plain:
            s = contract_cols(query, k_ref[: plain * BLOCK, :])
            scores.append((s, 0))
            tops.append(jnp.max(s, axis=1, keepdims=True))
        k0, k1 = first_masked * BLOCK, (qi + 1) * BLOCK
        s = contract_cols(query, k_ref[k0:k1, :])
        col_ids = k0 + lax.broadcasted_iota(jnp.int32, (1, k1 - k0), 1)
        visible = col_ids <= row_ids
        if qi >= prompt_blocks:
            visible = visible & (segc_ref[q0 : q0 + BLOCK, :] == segr_ref[:, k0:k1])
        s = jnp.where(visible, s, -1e30)
        scores.append((s, k0))
        tops.append(jnp.max(s, axis=1, keepdims=True))
        top = functools.reduce(jnp.maximum, tops)
        total, mixed = None, None
        for s, start in scores:
            p = jnp.exp(s - top)
            part = jnp.sum(p, axis=1, keepdims=True)
            total = part if total is None else total + part
            part = matmul(p.astype(BF16), v_ref[start : start + s.shape[1], :])
            mixed = part if mixed is None else mixed + part
        acc_ref[q0 : q0 + BLOCK, :] = jnp.where(
            keep, mixed / total, acc_ref[q0 : q0 + BLOCK, :]
        )
        lse = top + jnp.log(total)
        lse_ref[:, q0 : q0 + BLOCK] = jnp.broadcast_to(lse, (BLOCK, 128)).T[0:1, :]

    @pl.when(head == pl.num_programs(0) - 1)
    def _():
        o_ref[...] = acc_ref[...].astype(BF16)


def attend(query, key, value, seg_col, seg_row):
    tokens, width = query.shape
    heads = width // HEAD_DIM
    whole = lambda shape: pl.BlockSpec(shape, lambda h: (0, 0))
    return pl.pallas_call(
        attend_kernel,
        grid=(heads,),
        in_specs=[whole((tokens, width))] * 3 + [whole((tokens, 1)), whole((1, tokens))],
        out_specs=[
            whole((tokens, width)),
            pl.BlockSpec((pl.Squeezed(), 1, tokens), lambda h: (h, 0, 0)),
        ],
        out_shape=[
            jax.ShapeDtypeStruct((tokens, width), BF16),
            jax.ShapeDtypeStruct((heads, 1, tokens), F32),
        ],
        scratch_shapes=[pltpu.VMEM((tokens, width), BF16), pltpu.VMEM((tokens, width), F32)],
        compiler_params=pltpu.CompilerParams(vmem_limit_bytes=VMEM_LIMIT),
        cost_estimate=pl.CostEstimate(
            flops=9 << 30, bytes_accessed=8 << 20, transcendentals=9 << 20
        ),
        name="attend",
    )(query, key, value, seg_col, seg_row)


def attend_back_kernel(
    q_ref, k_ref, v_ref, do_ref, o_ref, lse_ref, segc_ref, segr_ref, cos_ref, sin_ref,
    grads_ref, first_ref, qh_ref, kh_ref, doh_ref, dq_ref, dk_ref, dv_ref,
):
    head = pl.program_id(0)
    tokens, width = q_ref.shape
    keep = jnp.where(head_lanes(width, head), 1.0, 0.0)
    keep_low = keep.astype(BF16)
    qh_ref[...] = q_ref[...] * (0.125 * keep).astype(BF16)
    kh_ref[...] = k_ref[...] * keep_low
    doh_ref[...] = do_ref[...] * keep_low
    prompt_blocks = PROMPT_LEN // BLOCK
    blocks = tokens // BLOCK

    @pl.when(head == 0)
    def _():
        dq_ref[...] = jnp.zeros_like(dq_ref)
        dk_ref[...] = jnp.zeros_like(dk_ref)
        dv_ref[...] = jnp.zeros_like(dv_ref)

    ones = jnp.ones((8, width), F32)
    deltas = []
    for qi in range(blocks):
        rows = slice(qi * BLOCK, (qi + 1) * BLOCK)
        product = o_ref[rows, :].astype(F32) * doh_ref[rows, :].astype(F32)
        deltas.append(
            lax.dot_general(
                ones, product, (((1,), (1,)), ((), ())),
                precision=lax.Precision.HIGHEST, preferred_element_type=F32,
            )[0:1, :]
        )

    for kj in range(blocks):
        k0 = kj * BLOCK
        keys = slice(k0, k0 + BLOCK)
        last = blocks if kj < prompt_blocks else min(kj + 2, blocks)
        key_ids = k0 + lax.broadcasted_iota(jnp.int32, (BLOCK, 1), 0)
        sum_k, sum_v = None, None
        for qi in range(kj, last):
            rows = slice(qi * BLOCK, (qi + 1) * BLOCK)
            s = contract_cols(k_ref[keys, :], qh_ref[rows, :])
            p = jnp.exp(s - lse_ref[:, rows])
            if qi == kj or kj >= prompt_blocks:
                query_ids = qi * BLOCK + lax.broadcasted_iota(jnp.int32, (1, BLOCK), 1)
                visible = key_ids <= query_ids
                if kj >= prompt_blocks:
                    visible = visible & (segc_ref[keys, :] == segr_ref[:, rows])
                p = jnp.where(visible, p, 0.0)
            dp = contract_cols(v_ref[keys, :], doh_ref[rows, :])
            ds = (p * (dp - deltas[qi])).astype(BF16)
            part_v = matmul(p.astype(BF16), doh_ref[rows, :])
            part_k = matmul(ds, qh_ref[rows, :])
            sum_v = part_v if sum_v is None else sum_v + part_v
            sum_k = part_k if sum_k is None else sum_k + part_k
            dq_ref[rows, :] += contract_rows(ds, kh_ref[keys, :])
        dk_ref[keys, :] += sum_k
        dv_ref[keys, :] += sum_v

    @pl.when(head == pl.num_programs(0) - 1)
    def _():
        for qi in range(blocks):
            rows = slice(qi * BLOCK, (qi + 1) * BLOCK)
            cosine, sine = cos_ref[rows, :], -sin_ref[rows, :]
            half_v = 0.5 * dv_ref[rows, :]
            first_ref[rows, :] = half_v
            grads_ref[rows, :width] = turn(0.125 * dq_ref[rows, :], cosine, sine).astype(BF16)
            grads_ref[rows, width : 2 * width] = turn(dk_ref[rows, :], cosine, sine).astype(BF16)
            grads_ref[rows, 2 * width :] = half_v.astype(BF16)


def attend_back(query, key, value, grad_out, out, lse, seg_col, seg_row, cosine, sine):
    tokens, width = query.shape
    heads = width // HEAD_DIM
    whole = lambda shape: pl.BlockSpec(shape, lambda h: (0, 0))
    wide = whole((tokens, width))
    return pl.pallas_call(
        attend_back_kernel,
        grid=(heads,),
        in_specs=[
            wide, wide, wide, wide, wide,
            pl.BlockSpec((pl.Squeezed(), 1, tokens), lambda h: (h, 0, 0)),
            whole((tokens, 1)), whole((1, tokens)), whole((tokens, 128)), whole((tokens, 128)),
        ],
        out_specs=[whole((tokens, 3 * width)), wide],
        out_shape=[
            jax.ShapeDtypeStruct((tokens, 3 * width), BF16),
            jax.ShapeDtypeStruct((tokens, width), F32),
        ],
        scratch_shapes=[pltpu.VMEM((tokens, width), BF16)] * 3
        + [pltpu.VMEM((tokens, width), F32)] * 3,
        compiler_params=pltpu.CompilerParams(vmem_limit_bytes=VMEM_LIMIT),
        cost_estimate=pl.CostEstimate(
            flops=22 << 30, bytes_accessed=14 << 20, transcendentals=9 << 20
        ),
        name="attend_back",
    )(query, key, value, grad_out, out, lse, seg_col, seg_row, cosine, sine)


def fill_out_kernel(at_ref, mine_ref, other_ref, full_ref):
    rings, pairs, rows, wide = mine_ref.shape
    core = at_ref[2]
    for ring in range(rings):
        head_row = lax.rem(at_ref[0] + rings - ring, rings) * (2 * rows)
        for pair in range(pairs):
            column = (at_ref[1] ^ pair) * wide
            for source, owner in ((mine_ref, core), (other_ref, 1 - core)):
                start = pl.multiple_of(column + owner * (wide // 2), wide // 2)
                for top in range(2):
                    row = pl.multiple_of(head_row + top * rows, rows)
                    full_ref[pl.ds(row, rows), pl.ds(start, wide // 2)] = source[
                        ring, pair, :, top * (wide // 2) : (top + 1) * (wide // 2)
                    ]


def fill_out(place, mine, other):
    rings, pairs, rows, wide = mine.shape
    return pl.pallas_call(
        fill_out_kernel,
        grid_spec=pltpu.PrefetchScalarGridSpec(
            num_scalar_prefetch=1,
            grid=(1,),
            in_specs=[pl.BlockSpec(mine.shape, lambda i, b: (0, 0, 0, 0))] * 2,
            out_specs=pl.BlockSpec((rings * rows * 2, pairs * wide), lambda i, b: (0, 0)),
        ),
        out_shape=jax.ShapeDtypeStruct((rings * rows * 2, pairs * wide), BF16),
        compiler_params=pltpu.CompilerParams(vmem_limit_bytes=VMEM_LIMIT),
        cost_estimate=pl.CostEstimate(flops=0, bytes_accessed=4 << 20, transcendentals=0),
        name="fill_out",
    )(place, mine, other)


def middle_kernel(a_ref, w_ref, x_ref, gain_ref, mid_ref, n_ref):
    middle = x_ref[...].astype(F32) + matmul(a_ref[...], w_ref[...])
    mid_ref[...] = middle
    inverse = lax.rsqrt(jnp.mean(middle * middle, axis=1, keepdims=True) + epsilon)
    n_ref[...] = (middle * inverse * gain_ref[...]).astype(BF16)


def middle_rows(attended, out_full, hidden_in, gain):
    rows, model = hidden_in.shape
    step = 256
    row = pl.BlockSpec((step, model), lambda i: (i, 0))
    return pl.pallas_call(
        middle_kernel,
        grid=(rows // step,),
        in_specs=[
            row, pl.BlockSpec(out_full.shape, lambda i: (0, 0)), row,
            pl.BlockSpec((1, model), lambda i: (0, 0)),
        ],
        out_specs=[row, row],
        out_shape=[
            jax.ShapeDtypeStruct((rows, model), F32), jax.ShapeDtypeStruct((rows, model), BF16),
        ],
        compiler_params=pltpu.CompilerParams(vmem_limit_bytes=VMEM_LIMIT),
        cost_estimate=pl.CostEstimate(
            flops=2 * rows * model * model, bytes_accessed=7 << 20, transcendentals=0
        ),
        name="middle",
    )(attended, out_full, hidden_in, gain)


def middle_back_kernel(d_ref, r_ref, mid_ref, c_ref, gain_ref, w_ref, gm_ref, low_ref, ga_ref, gg_ref):
    middle = mid_ref[...]
    inverse = lax.rsqrt(jnp.mean(middle * middle, axis=1, keepdims=True) + epsilon)
    scaled = middle * inverse
    grad = d_ref[...] + r_ref[...].astype(F32)
    part = jnp.sum(grad * scaled, axis=0, keepdims=True)

    @pl.when(pl.program_id(0) == 0)
    def _():
        gg_ref[...] = part

    @pl.when(pl.program_id(0) != 0)
    def _():
        gg_ref[...] += part

    weighted = grad * gain_ref[...]
    grad_middle = c_ref[...].astype(F32) + inverse * (
        weighted - scaled * jnp.mean(weighted * scaled, axis=1, keepdims=True)
    )
    gm_ref[...] = grad_middle
    low = grad_middle.astype(BF16)
    low_ref[...] = low
    ga_ref[...] = contract_cols(low, w_ref[...]).astype(BF16)


def middle_back(grad_own, arrived, middle, cotangent, gain, out_full):
    rows, model = middle.shape
    step = 256
    row = pl.BlockSpec((step, model), lambda i: (i, 0))
    one = pl.BlockSpec((1, model), lambda i: (0, 0))
    return pl.pallas_call(
        middle_back_kernel,
        grid=(rows // step,),
        in_specs=[row, row, row, row, one, pl.BlockSpec(out_full.shape, lambda i: (0, 0))],
        out_specs=[row, row, row, one],
        out_shape=[
            jax.ShapeDtypeStruct((rows, model), F32),
            jax.ShapeDtypeStruct((rows, model), BF16),
            jax.ShapeDtypeStruct((rows, out_full.shape[0]), BF16),
            jax.ShapeDtypeStruct((1, model), F32),
        ],
        compiler_params=pltpu.CompilerParams(vmem_limit_bytes=VMEM_LIMIT),
        cost_estimate=pl.CostEstimate(
            flops=2 * rows * model * model, bytes_accessed=12 << 20, transcendentals=0
        ),
        name="middle_back",
    )(grad_own, arrived, middle, cotangent, gain, out_full)


def block_copies(place_ref, blocks, target, sems, first_row, rows, pairs):
    wide = target.shape[1] // pairs
    copies = []
    for index, block in enumerate(blocks):
        ring, pair = divmod(index, pairs)
        start = 0 if pairs == 1 else pl.multiple_of((place_ref[1] ^ pair) * wide, wide)
        copies.append(
            pltpu.make_async_copy(
                block.at[pl.ds(first_row, rows), :],
                target.at[pl.ds(ring * rows, rows), pl.ds(start, wide)],
                sems.at[index],
            )
        )
    return copies


def ffn_kernel(pairs, half, place_ref, n0_ref, n1_ref, c0_ref, c1_ref, *rest):
    count = len(rest) - 9
    blocks = rest[:count]
    dx0_ref, dx1_ref, h_ref, ht_ref, gt_ref, ut_ref, full_ref, sems = rest[count : count + 8]
    step_id = pl.program_id(0)
    rows_of = rest[-1]
    order = (0, 1, 2)

    def copies(which):
        return block_copies(
            place_ref, blocks, full_ref.at[which], sems.at[which], which * half, half, pairs
        )

    @pl.when(step_id == 0)
    def _():
        for which in order:
            for copy in copies(which):
                copy.start()
        for which in order:
            for copy in copies(which):
                copy.wait()

    mine = step_id < pl.num_programs(0) // 2
    rows_of[0] = jnp.where(mine, n0_ref[...], n1_ref[...])
    rows_of[1] = jnp.where(mine, c0_ref[...], c1_ref[...])
    normed, cot = rows_of[0], rows_of[1]
    gate = contract_cols(normed, full_ref[0])
    up = contract_cols(normed, full_ref[1])
    grad = contract_cols(cot, full_ref[2])
    sig = jax.nn.sigmoid(gate)
    silu = gate * sig
    hidden = (silu * up).astype(BF16)
    grad_up = (grad * silu).astype(BF16)
    grad_gate = (grad * up * sig * (1.0 + gate * (1.0 - sig))).astype(BF16)
    h_ref[...] = hidden
    ht_ref[...] = hidden.T
    gt_ref[...] = grad_gate.T
    ut_ref[...] = grad_up.T
    dx = matmul(grad_gate, full_ref[0]) + matmul(grad_up, full_ref[1])

    @pl.when(mine)
    def _():
        dx0_ref[...] = dx

    @pl.when(jnp.logical_not(mine))
    def _():
        dx1_ref[...] = dx.astype(BF16)


def ffn(place, normed, normed_other, cot, cot_other, blocks, half, pairs):
    rows, model = normed.shape
    step = 256
    each = rows // step
    rings = len(blocks) // pairs
    units = half * rings
    own = pl.BlockSpec((step, model), lambda i, b: (jnp.minimum(i, each - 1), 0))
    other = pl.BlockSpec((step, model), lambda i, b: (jnp.maximum(i - each, 0), 0))
    turned = pl.BlockSpec((units, step), lambda i, b: (0, i))
    return pl.pallas_call(
        functools.partial(ffn_kernel, pairs, half),
        grid_spec=pltpu.PrefetchScalarGridSpec(
            num_scalar_prefetch=1,
            grid=(2 * each,),
            in_specs=[own, other, own, other]
            + [pl.BlockSpec(memory_space=pl.ANY)] * len(blocks),
            out_specs=[
                own, other, pl.BlockSpec((step, units), lambda i, b: (i, 0)),
                turned, turned, turned,
            ],
            scratch_shapes=[
                pltpu.VMEM((3, units, model), BF16),
                pltpu.SemaphoreType.DMA((3, len(blocks))),
                pltpu.VMEM((2, step, model), BF16),
            ],
        ),
        out_shape=[
            jax.ShapeDtypeStruct((rows, model), F32),
            jax.ShapeDtypeStruct((rows, model), BF16),
            jax.ShapeDtypeStruct((2 * rows, units), BF16),
        ]
        + [jax.ShapeDtypeStruct((units, 2 * rows), BF16)] * 3,
        compiler_params=pltpu.CompilerParams(vmem_limit_bytes=VMEM_LIMIT),
        cost_estimate=pl.CostEstimate(
            flops=20 * rows * model * units, bytes_accessed=30 << 20, transcendentals=2 << 20
        ),
        name="ffn",
    )(place, normed, normed_other, cot, cot_other, *blocks)


def ffn_out_kernel(pairs, half, place_ref, h_ref, *rest):
    blocks = rest[:-4]
    own_ref, other_ref, full_ref, sems = rest[-4:]

    @pl.when(pl.program_id(0) == 0)
    def _():
        all_copies = block_copies(place_ref, blocks, full_ref, sems, 2 * half, half, pairs)
        for copy in all_copies:
            copy.start()
        for copy in all_copies:
            copy.wait()

    out = matmul(h_ref[...], full_ref[...])
    mine = pl.program_id(0) < pl.num_programs(0) // 2

    @pl.when(mine)
    def _():
        own_ref[...] = out

    @pl.when(jnp.logical_not(mine))
    def _():
        other_ref[...] = out.astype(BF16)


def ffn_out(place, hidden, blocks, half, pairs, model):
    both, units = hidden.shape
    rows = both // 2
    step = 256
    each = rows // step
    own = pl.BlockSpec((step, model), lambda i, b: (jnp.minimum(i, each - 1), 0))
    other = pl.BlockSpec((step, model), lambda i, b: (jnp.maximum(i - each, 0), 0))
    return pl.pallas_call(
        functools.partial(ffn_out_kernel, pairs, half),
        grid_spec=pltpu.PrefetchScalarGridSpec(
            num_scalar_prefetch=1,
            grid=(2 * each,),
            in_specs=[pl.BlockSpec((step, units), lambda i, b: (i, 0))]
            + [pl.BlockSpec(memory_space=pl.ANY)] * len(blocks),
            out_specs=[own, other],
            scratch_shapes=[
                pltpu.VMEM((units, model), BF16), pltpu.SemaphoreType.DMA((len(blocks),)),
            ],
        ),
        out_shape=[
            jax.ShapeDtypeStruct((rows, model), F32), jax.ShapeDtypeStruct((rows, model), BF16),
        ],
        compiler_params=pltpu.CompilerParams(vmem_limit_bytes=VMEM_LIMIT),
        cost_estimate=pl.CostEstimate(
            flops=4 * rows * model * units, bytes_accessed=9 << 20, transcendentals=0
        ),
        name="ffn_out",
    )(place, hidden, *blocks)


def ffn_weights_kernel(half, col_ref, gt_ref, ut_ref, ht_ref, n0_ref, n1_ref, c0_ref, c1_ref, *outs):
    rows = n0_ref.shape[0]
    for which, (left, r0, r1) in enumerate(
        ((gt_ref, n0_ref, n1_ref), (ut_ref, n0_ref, n1_ref), (ht_ref, c0_ref, c1_ref))
    ):
        for ring, out in enumerate(outs):
            units = slice(ring * half, (ring + 1) * half)
            grad = matmul(left[units, :rows], r0[...]) + matmul(left[units, rows:], r1[...])
            out[which * half : (which + 1) * half, :] = grad.astype(BF16)


def ffn_weights(column, wide, half, grad_gate, grad_up, hidden, normed, normed_other, cot, cot_other):
    units, both = hidden.shape
    rows = both // 2
    whole = pl.BlockSpec((units, both), lambda i, c: (0, 0))
    block = pl.BlockSpec((rows, wide), lambda i, c: (0, c[0]))
    rings = units // half
    return pl.pallas_call(
        functools.partial(ffn_weights_kernel, half),
        grid_spec=pltpu.PrefetchScalarGridSpec(
            num_scalar_prefetch=1,
            grid=(1,),
            in_specs=[whole] * 3 + [block] * 4,
            out_specs=[pl.BlockSpec((3 * half, wide), lambda i, c: (0, 0))] * rings,
        ),
        out_shape=[jax.ShapeDtypeStruct((3 * half, wide), BF16)] * rings,
        compiler_params=pltpu.CompilerParams(vmem_limit_bytes=VMEM_LIMIT),
        cost_estimate=pl.CostEstimate(
            flops=6 * both * units * wide, bytes_accessed=13 << 20, transcendentals=0
        ),
        name="ffn_weights",
    )(column, grad_gate, grad_up, hidden, normed, normed_other, cot, cot_other)


def add_low(left, right):
    return (left.astype(F32) + right.astype(F32)).astype(BF16)


def on_device(
    hidden_in, value_first, segment_ids, gain_attn, w_query, w_key, w_value, w_out,
    gain_ffn, w_gate, w_up, w_down, cotangent, *, chips, depth,
):
    swap = lambda v: lax.ppermute(v, "core", [(0, 1), (1, 0)])
    onward = lambda v: lax.ppermute(v, "tensor", [(i, (i + 1) % depth) for i in range(depth)])
    across = lambda v, bit: lax.ppermute(v, "chip", [(i, i ^ bit) for i in range(chips)])
    rows, model = hidden_in.shape
    part = w_query.shape[0]
    units = w_gate.shape[1]
    half = units // 2
    heads_wide = w_query.shape[1]
    fast = chips == 4 and part == 128
    pairs = chips if fast else 1
    place = jnp.stack(
        [lax.axis_index("tensor"), lax.axis_index("chip"), lax.axis_index("core")]
    ).astype(jnp.int32)
    ring_block = lambda k: lax.rem(place[:1] + (depth - k), depth)

    x_parts = [hidden_in]
    for _ in range(depth - 1):
        x_parts.append(onward(x_parts[-1]))
    w_qkv = lax.all_gather(
        jnp.concatenate([w_query, w_key, w_value], axis=1), ("chip", "core"), axis=0, tiled=True
    )

    mlp_local = jnp.concatenate([w_gate.T, w_up.T, w_down]).reshape(3, 2, half, part)
    mlp_local = lax.all_to_all(mlp_local, "core", 1, 3, tiled=True).reshape(3 * half, 2 * part)
    if fast:
        out_local = jnp.concatenate([w_out[:part], w_out[part:]], axis=1)
        local = jnp.concatenate([mlp_local, out_local])
    else:
        local = lax.all_gather(mlp_local, "chip", axis=1, tiled=True)
    slots = [local]
    for _ in range(depth - 1):
        slots.append(onward(slots[-1]))
    if fast:
        blocks = []
        for k, slot in enumerate(slots):
            low, high = (1, 2) if k % 2 == 0 else (2, 1)
            near, far = across(slot, low), across(slot, high)
            group = {0: slot, low: near, high: far, 3: across(near, high)}
            blocks.extend(group[r] for r in range(4))
        mine = jnp.stack([b[3 * half :] for b in blocks]).reshape(depth, pairs, part, 2 * part)
        out_full = fill_out(place, mine, swap(mine))
    else:
        blocks = slots
        out_parts = lax.all_gather(w_out, ("chip", "core", "tensor"), axis=0)
        out_full = (
            out_parts.reshape(2 * chips, depth, heads_wide, part)
            .transpose(1, 2, 0, 3)
            .reshape(depth * heads_wide, model)
        )

    position = token_positions(segment_ids)
    cosine, sine = rotation_tables(position)
    seg_col, seg_row = segment_ids.reshape(-1, 1), segment_ids.reshape(1, -1)
    gain_one, gain_two = gain_attn.reshape(1, model), gain_ffn.reshape(1, model)
    filled = ()
    for k, x_part in enumerate(x_parts):
        filled = project(ring_block(k), filled, x_part, w_qkv, gain_one, cosine, sine, value_first)
    normed_all, query, key, value = filled
    mixed, lse = attend(query, key, value, seg_col, seg_row)
    attended = lax.all_to_all(mixed, "tensor", 0, 1, tiled=True)

    middle, normed = middle_rows(attended, out_full, hidden_in, gain_two)
    normed_other, cot_other = swap(normed), swap(cotangent)
    grad_own, grad_other, hidden, hidden_t, gate_t, up_t = ffn(
        place, normed, normed_other, cotangent, cot_other, blocks, half, pairs
    )
    grad_middle, grad_low, grad_att, gain_two_part = middle_back(
        grad_own, swap(grad_other), middle, cotangent, gain_two, out_full
    )
    grad_mixed = lax.all_to_all(grad_att, "tensor", 1, 0, tiled=True)

    out_own, out_other = ffn_out(place, hidden, blocks, half, pairs, model)
    output = (middle + out_own + swap(out_other).astype(F32)).astype(BF16)

    terms = {}
    for r in (3, 1, 2, 0) if fast else (0,):
        column = (place[1:2] ^ r) if fast else jnp.zeros((1,), jnp.int32)
        terms[r] = ffn_weights(
            column, model // pairs, half, gate_t, up_t, hidden_t,
            normed, normed_other, cotangent, cot_other,
        )
    sums = []
    for k in range(depth):
        if fast:
            low, high = (1, 2) if k % 2 == 0 else (2, 1)
            own = add_low(terms[low][k], across(terms[3][k], high))
            first = add_low(terms[0][k], across(terms[high][k], high))
            sums.append(add_low(first, across(own, low)))
        else:
            spread = terms[0][k].reshape(3 * half, chips, 2 * part).transpose(1, 0, 2)
            sums.append(lax.psum_scatter(spread, "chip", scatter_dimension=0))
    total = sums[1 % depth]
    for k in range(2, depth + 1):
        total = add_low(sums[k % depth], onward(total))
    mlp_sum = lax.all_to_all(
        total.reshape(3, 1, half, 2 * part), "core", 3, 1, tiled=True
    ).reshape(3, units, part).astype(F32)

    out_grad = (
        contract_rows(attended, grad_low)
        .astype(BF16)
        .reshape(depth * heads_wide, 2 * chips, part)
        .transpose(1, 0, 2)
    )
    out_sum = lax.psum_scatter(
        lax.psum_scatter(out_grad, ("chip", "core"), scatter_dimension=0),
        "tensor",
        scatter_dimension=0,
        tiled=True,
    )

    qkv_grads, grad_value_first = attend_back(
        query, key, value, grad_mixed, mixed, lse, seg_col, seg_row, cosine, sine
    )
    arrived, gain_one_part = None, 0.0
    for k in range(1, depth + 1):
        final = grad_middle if k == depth else None
        back, gain_term = unproject(
            ring_block(k % depth), qkv_grads, w_qkv, x_parts[k % depth], gain_one, arrived, final
        )
        gain_one_part = gain_one_part + gain_term
        if k < depth:
            arrived = onward(back)
    grad_input = back
    qkv_sum = lax.psum_scatter(
        contract_rows(normed_all, qkv_grads).astype(BF16),
        ("chip", "core"),
        scatter_dimension=0,
        tiled=True,
    ).astype(F32)
    devices = 2 * chips * depth
    gains = jnp.concatenate([gain_one_part, gain_two_part]).reshape(2, devices, -1).transpose(1, 0, 2)
    gains = jnp.sum(
        lax.all_to_all(gains, ("chip", "core", "tensor"), 0, 0, tiled=True), axis=0
    )
    return (
        output,
        grad_input,
        grad_value_first,
        gains[0],
        qkv_sum[:, :heads_wide],
        qkv_sum[:, heads_wide : 2 * heads_wide],
        qkv_sum[:, 2 * heads_wide :],
        out_sum.astype(F32),
        gains[1],
        mlp_sum[0].T,
        mlp_sum[1].T,
        mlp_sum[2],
    )


def solution(mesh):
    dp, depth = mesh.shape["dp"], mesh.shape["tensor"]
    chips = dp // 2
    fine = Mesh(mesh.devices.reshape(chips, 2, depth), ("chip", "core", "tensor"))
    every = ("chip", "core", "tensor")
    split = ("chip", "core")
    return jax.shard_map(
        functools.partial(on_device, chips=chips, depth=depth),
        mesh=fine,
        in_specs=(
            P(every, None), P(split, "tensor"), P(split), P(),
            P(split, "tensor"), P(split, "tensor"), P(split, "tensor"), P("tensor", split),
            P(), P(split, "tensor"), P(split, "tensor"), P("tensor", split), P(every, None),
        ),
        out_specs=(
            P(every, None), P(every, None), P(split, "tensor"), P(every),
            P(split, "tensor"), P(split, "tensor"), P(split, "tensor"), P("tensor", split),
            P(every), P(split, "tensor"), P(split, "tensor"), P("tensor", split),
        ),
        check_vma=False,
    )
```

time: 1400 us -> 517 us (0.37)
  waiting for transfers between devices: 817 us -> 174 us
  matrix products: 269 us -> 8.17 us
  Pallas kernels: 0 us -> 191 us
  blocking collectives: 84.8 us -> 4.52 us
  other arithmetic: 101 us -> 27.1 us
  local copies, waits for them, and re-layouts: 93.2 us -> 39.3 us
  starting transfers between devices: 1.16 us -> 51.2 us
    reduce_scatter x11 -> x3, waiting for transfers between devices: 499 us -> 0.02 us  [the longest x1 0.02 us: on_device(): lax.psum_scatter(contract_rows(normed_all, qkv_grads).astype(BF16), ('chi...]
    all_gather x7 -> x1, waiting for transfers between devices: 315 us -> 0.01 us  [on_device(): lax.all_gather(jnp.concatenate([w_query, w_key, w_value], axis=1), ('chip...]
    dot_general x42 -> x0, matrix products: 227 us -> none  [the longest x4 46.4 us: one_block(): jnp.einsum('qhd,khd->hqk', grad_heads, value_heads, preferred_element_typ...]
    pallas_call x0 -> x19, Pallas kernels: none -> 191 us  [the longest x1 54 us: attend_back(): pl.pallas_call(attend_back_kernel, grid=(heads,), in_specs=[wide, wide, w...]
    ppermute x0 -> x41, waiting for transfers between devices: none -> 155 us  [the longest x12 114 us: on_device(): lax.ppermute(v, 'tensor', [(i, (i + 1) % depth) for i in range(depth)])]
    dynamic_update_slice x16 -> x0, local copies, waits for them, and re-layouts: 49.7 us -> none  [the longest x8 46.3 us: attention_backward(): lax.scan(one_block, (zero_carry, zero_carry), inputs)]
    unnamed x1 -> x0, blocking collectives: 42.9 us -> none
    all_gather x4 -> x0, blocking collectives: 41.9 us -> none  [the longest x1 11.3 us: on_device(): lax.all_gather(w_query, 'dp', axis=0, tiled=True)]
  transfers between devices with their start and end apart: 18 -> 49, of which waited for: 16 -> 16; matrix products, arithmetic and copies ran while one was open for 7% -> 13% of each run, Pallas kernels for 0% -> 30%
where the time goes in v1:
time: 517 us; the launch traced here: 510 us
  Pallas kernels  191 us (37%)
  waiting for transfers between devices  174 us (34%)
  starting transfers between devices  51.2 us (10%)
  local copies, waits for them, and re-layouts  39.3 us (8%)
  other arithmetic  27.1 us (5%)
  between operations  14.5 us (3%)
  matrix products  8.17 us (2%)
    ppermute x12, waiting for transfers between devices, on_device(): lax.ppermute(v, 'tensor', [(i, (i + 1) % depth) for i in range(depth)])  114 us
    pallas_call x1, Pallas kernels, attend_back(): pl.pallas_call(attend_back_kernel, grid=(heads,), in_specs=[wide, wide, w...  54 us
    ppermute x24, waiting for transfers between devices, on_device(): lax.ppermute(v, 'chip', [(i, i ^ bit) for i in range(chips)])  35.1 us
    pallas_call x4, Pallas kernels, ffn_weights(): pl.pallas_call(functools.partial(ffn_weights_kernel, half), grid_spec=plt...  28.4 us
    pallas_call x1, Pallas kernels, ffn(): pl.pallas_call(functools.partial(ffn_kernel, pairs, half), grid_spec=pltp...  27.2 us
    ppermute x24, starting transfers between devices, on_device(): lax.ppermute(v, 'chip', [(i, i ^ bit) for i in range(chips)])  26.7 us
    unnamed x95, local copies, waits for them, and re-layouts  22 us
    pallas_call x1, Pallas kernels, attend(): pl.pallas_call(attend_kernel, grid=(heads,), in_specs=[whole((tokens, wid...  21.7 us
  transfers between devices with their start and end apart: 49, of which 16 were waited for; matrix products, arithmetic and copies ran while one was open for 13% of the time, Pallas kernels for 30%

profile of v1, /device:TPU:0, one launch (start us, length us, event | category | flops | bytes accessed | tf_op | source)
XLA Modules:
  0.0 509.5 jit_solution(16679049143787854782)
XLA Ops:
  27.5 10.5 %collective-permute-done.6.rest_4_ = bf16[1184,256]{1,0:T(8,128)(2,1)} collective-permute-done((bf16[1184,256]{1,0:T(8,128)(2,1)S(1)}, bf16[1184,256]{1,0:T(8,128)(2,1)}, u32[]{:S(2)}, u32[]{:S(2)}) %collective-permute-start.6) | collective-permute-done | bytes 606240 | tf_op jit(solution)/shard_map/ppermute | solution.py:648
  47.8 12.6 %collective-permute-done.x_ref = bf16[512,1024]{1,0:T(8,128)(2,1)S(1)} collective-permute-done((bf16[512,1024]{1,0:T(8,128)(2,1)S(1)}, bf16[512,1024]{1,0:T(8,128)(2,1)S(1)}, u32[]{:S(2)}, u32[]{:S(2)}) %collective-permute-start) | collective-permute-done | bytes 1048608 | tf_op jit(solution)/shard_map/ppermute | solution.py:648
  60.4 13.1 %collective-permute-done.10.rest_8_ = bf16[1184,256]{1,0:T(8,128)(2,1)} collective-permute-done((bf16[1184,256]{1,0:T(8,128)(2,1)}, bf16[1184,256]{1,0:T(8,128)(2,1)}, u32[]{:S(2)}, u32[]{:S(2)}) %collective-permute-start.10) | collective-permute-done | bytes 606240 | tf_op jit(solution)/shard_map/ppermute | solution.py:648
  81.2 26.4 %collective-permute-done.14.rest_12_ = bf16[1184,256]{1,0:T(8,128)(2,1)} collective-permute-done((bf16[1184,256]{1,0:T(8,128)(2,1)}, bf16[1184,256]{1,0:T(8,128)(2,1)}, u32[]{:S(2)}, u32[]{:S(2)}) %collective-permute-start.14) | collective-permute-done | bytes 606240 | tf_op jit(solution)/shard_map/ppermute | solution.py:648
  114.0 11.1 %collective-permute-done.16.rest_14_ = bf16[1184,256]{1,0:T(8,128)(2,1)} collective-permute-done((bf16[1184,256]{1,0:T(8,128)(2,1)}, bf16[1184,256]{1,0:T(8,128)(2,1)}, u32[]{:S(2)}, u32[]{:S(2)}) %collective-permute-start.16) | collective-permute-done | bytes 606240 | tf_op jit(solution)/shard_map/ppermute | solution.py:649
  126.6 8.8 %collective-permute-done.13.rest_11_ = bf16[1184,256]{1,0:T(8,128)(2,1)S(1)} collective-permute-done((bf16[1184,256]{1,0:T(8,128)(2,1)S(1)}, bf16[1184,256]{1,0:T(8,128)(2,1)S(1)}, u32[]{:S(2)}, u32[]{:S(2)}) %collective-permute-start.13) | collective-permute-done | bytes 606240 | tf_op jit(solution)/shard_map/ppermute | solution.py:649
  137.7 4.1 project.4
  145.8 4.1 project.6
  155.0 21.7 %attend.1 = (bf16[2048,256]{1,0:T(8,128)(2,1)}, f32[4,1,2048]{2,1,0:T(1,128)}) custom-call(bf16[2048,256]{1,0:T(8,128)(2,1)} %get-tuple-element.82.q_ref, bf16[2048,256]{1,0:T(8,128)(2,1)} %get-tuple-element.83.k_ref, bf16[2048,256]{1,0:T(8,128)(2,1)} %get-tuple-element.84.v_ref, s32[2048,1]{1,0:T(8,128)} %copy.85.segc_ref, s32[1,2048]{1,0:T(1,128)} %bitcast.149), custom_call_target="tpu_custom_call" | custom-call | flops 9663676416 | bytes 8388608 | tf_op jit(solution)/shard_map/attend/pallas_call | solution.py:215
  176.7 4.2 all-to-all-start
  189.7 4.1 fill_out.1.w_ref
  193.8 10.8 %all-to-all-done = bf16[4,512,256]{2,1,0:T(8,128)(2,1)S(1)} async-done(((bf16[4,512,256]{2,1,0:T(8,128)(2,1)}), bf16[4,512,256]{2,1,0:T(8,128)(2,1)S(1)}, u32[]{:S(2)}, u32[]{:S(2)}) %all-to-all-start) | async-done | bytes 1048608 | tf_op jit(solution)/shard_map/all_to_all | solution.py:706
  205.7 4.7 middle.1
  214.2 27.2 %ffn.1 = (f32[512,1024]{1,0:T(8,128)}, bf16[512,1024]{1,0:T(8,128)(2,1)}, bf16[1024,1408]{1,0:T(8,128)(2,1)}, bf16[1408,1024]{1,0:T(8,128)(2,1)}, bf16[1408,1024...) custom-call(s32[3]{0:T(128)} %pad_add_fusion.at_ref.place_ref, bf16[512,1024]{1,0:T(8,128)(2,1)} %get-tuple-element.87.n0_ref, ...), custom_call_target="tpu_custom_call" | custom-call | flops 14763950080 | bytes 31457280 | tf_op jit(solution)/shard_map/ffn/pallas_call | solution.py:520
  241.4 9.8 %ffn_out.1 = (f32[512,1024]{1,0:T(8,128)}, bf16[512,1024]{1,0:T(8,128)(2,1)}) custom-call(s32[3]{0:T(128)} %pad_add_fusion.at_ref.place_ref, bf16[1024,1408]{1,0:T(8,128)(2,1)} %get-tuple-element.88.h_ref, bf16[1184,256]{1,0:T(8,128)(2,1)} %copy-done.10, bf16[1184,256]{1,0:T(8,128)(2,1)} %copy-done.16, bf16[1184,256]{1,0:T(8,128)(2,1)} %collective-permute-done.4.rest_2_, ...), custom_call_target="tpu_custom_call" | custom-call | flops 2952790016 | bytes 9437184 | tf_op jit(solution)/shard_map/ffn_out/pallas_call | solution.py:582
  251.9 7.1 %ffn_weights.7 = (bf16[1056,256]{1,0:T(8,128)(2,1)}, bf16[1056,256]{1,0:T(8,128)(2,1)}, bf16[1056,256]{1,0:T(8,128)(2,1)}, bf16[1056,256]{1,0:T(8,128)(2,1)}) custom-call(s32[1]{0:T(128)S(6)} %xor.11.col_ref, bf16[1408,1024]{1,0:T(8,128)(2,1)} %get-tuple-element.109.gt_ref, bf16[1408,1024]{1,0:T(8,128)(2,1)} %get-tuple-element.110.ut_ref, ...), custom_call_target="tpu_custom_call" | custom-call | flops 2214592512 | bytes 13631488 | tf_op jit(solution)/shard_map/ffn_weights/pallas_call | solution.py:622
  260.5 7.1 %ffn_weights.6 = (bf16[1056,256]{1,0:T(8,128)(2,1)}, bf16[1056,256]{1,0:T(8,128)(2,1)}, bf16[1056,256]{1,0:T(8,128)(2,1)}, bf16[1056,256]{1,0:T(8,128)(2,1)}) custom-call(s32[1]{0:T(128)S(6)} %xor.10.col_ref, bf16[1408,1024]{1,0:T(8,128)(2,1)} %get-tuple-element.109.gt_ref, bf16[1408,1024]{1,0:T(8,128)(2,1)} %get-tuple-element.110.ut_ref, ...), custom_call_target="tpu_custom_call" | custom-call | flops 2214592512 | bytes 13631488 | tf_op jit(solution)/shard_map/ffn_weights/pallas_call | solution.py:622
  269.1 7.1 %ffn_weights.4 = (bf16[1056,256]{1,0:T(8,128)(2,1)}, bf16[1056,256]{1,0:T(8,128)(2,1)}, bf16[1056,256]{1,0:T(8,128)(2,1)}, bf16[1056,256]{1,0:T(8,128)(2,1)}) custom-call(s32[1]{0:T(128)} %bitcast.6.col_ref, bf16[1408,1024]{1,0:T(8,128)(2,1)} %get-tuple-element.109.gt_ref, bf16[1408,1024]{1,0:T(8,128)(2,1)} %get-tuple-element.110.ut_ref, ...), custom_call_target="tpu_custom_call" | custom-call | flops 2214592512 | bytes 13631488 | tf_op jit(solution)/shard_map/ffn_weights/pallas_call | solution.py:622
  276.2 7.1 %ffn_weights.5 = (bf16[1056,256]{1,0:T(8,128)(2,1)}, bf16[1056,256]{1,0:T(8,128)(2,1)}, bf16[1056,256]{1,0:T(8,128)(2,1)}, bf16[1056,256]{1,0:T(8,128)(2,1)}) custom-call(s32[1]{0:T(128)S(6)} %xor.9.col_ref, bf16[1408,1024]{1,0:T(8,128)(2,1)} %get-tuple-element.109.gt_ref, bf16[1408,1024]{1,0:T(8,128)(2,1)} %get-tuple-element.110.ut_ref, ...), custom_call_target="tpu_custom_call" | custom-call | flops 2214592512 | bytes 13631488 | tf_op jit(solution)/shard_map/ffn_weights/pallas_call | solution.py:622
  287.9 6.1 %middle_back.1 = (f32[512,1024]{1,0:T(8,128)}, bf16[512,1024]{1,0:T(8,128)(2,1)}, bf16[512,1024]{1,0:T(8,128)(2,1)}, f32[1,1024]{1,0:T(1,128)}) custom-call(f32[512,1024]{1,0:T(8,128)} %get-tuple-element.91.d_ref, bf16[512,1024]{1,0:T(8,128)(2,1)} %copy-done.14, f32[512,1024]{1,0:T(8,128)} %get-tuple-element.86.mid_ref, bf16[512,1024]{1,0:T(8,128)(2,1)} %c0_ref.9, ...), custom_call_target="tpu_custom_call" | custom-call | flops 1073741824 | bytes 12582912 | tf_op jit(solution)/shard_map/middle_back/pallas_call | solution.py:427
  309.7 15.2 %collective-permute-done.37 = bf16[1056,256]{1,0:T(8,128)(2,1)} collective-permute-done((bf16[1056,256]{1,0:T(8,128)(2,1)}, bf16[1056,256]{1,0:T(8,128)(2,1)}, u32[]{:S(2)}, u32[]{:S(2)}) %collective-permute-start.37) | collective-permute-done | bytes 540704 | tf_op jit(solution)/shard_map/ppermute | solution.py:649
  329.0 54.0 %attend_back.1 = (bf16[2048,768]{1,0:T(8,128)(2,1)}, f32[2048,256]{1,0:T(8,128)}) custom-call(bf16[2048,256]{1,0:T(8,128)(2,1)} %get-tuple-element.82.q_ref, bf16[2048,256]{1,0:T(8,128)(2,1)} %get-tuple-element.83.k_ref, bf16[2048,256]{1,0:T(8,128)(2,1)} %get-tuple-element.84.v_ref, bf16[2048,256]{1,0:T(8,128)(2,1)} %bitcast.133, ...), custom_call_target="tpu_custom_call" | custom-call | flops 23622320128 | bytes 14680064 | tf_op jit(solution)/shard_map/attend_back/pallas_call | solution.py:311
  396.3 18.8 %collective-permute-done.23.rest_0_ = bf16[512,1024]{1,0:T(8,128)(2,1)S(1)} collective-permute-done((bf16[512,1024]{1,0:T(8,128)(2,1)}, bf16[512,1024]{1,0:T(8,128)(2,1)S(1)}, u32[]{:S(2)}, u32[]{:S(2)}) %collective-permute-start.23) | collective-permute-done | bytes 1048608 | tf_op jit(solution)/shard_map/ppermute | solution.py:648
  416.1 4.5 unproject.5
  420.7 6.9 %convolution_convert_fusion.1 = bf16[1024,768]{1,0:T(8,128)(2,1)} fusion(bf16[2048,1024]{1,0:T(8,128)(2,1)} %get-tuple-element.107, bf16[2048,768]{1,0:T(8,128)(2,1)S(1)} %copy-done), kind=kOutput, calls=%fused_computation.2 | convolution fusion | flops 3222011904 | bytes 8912896 | tf_op jit(solution)/shard_map/dot_general | solution.py:44
  435.8 17.8 %collective-permute-done.24.rest_0_ = bf16[512,1024]{1,0:T(8,128)(2,1)} collective-permute-done((bf16[512,1024]{1,0:T(8,128)(2,1)}, bf16[512,1024]{1,0:T(8,128)(2,1)}, u32[]{:S(2)}, u32[]{:S(2)}) %collective-permute-start.24) | collective-permute-done | bytes 1048608 | tf_op jit(solution)/shard_map/ppermute | solution.py:648
  453.5 4.6 unproject.6
  458.1 6.9 %collective-permute-done.40 = bf16[1056,256]{1,0:T(8,128)(2,1)S(1)} collective-permute-done((bf16[1056,256]{1,0:T(8,128)(2,1)S(1)}, bf16[1056,256]{1,0:T(8,128)(2,1)S(1)}, u32[]{:S(2)}, u32[]{:S(2)}) %collective-permute-start.40) | collective-permute-done | bytes 540704 | tf_op jit(solution)/shard_map/ppermute | solution.py:648
  465.9 4.5 all_to_all.67
  476.1 8.0 %collective-permute-done.25.rest_0_ = bf16[512,1024]{1,0:T(8,128)(2,1)S(1)} collective-permute-done((bf16[512,1024]{1,0:T(8,128)(2,1)}, bf16[512,1024]{1,0:T(8,128)(2,1)S(1)}, u32[]{:S(2)}, u32[]{:S(2)}) %collective-permute-start.25) | collective-permute-done | bytes 1048608 | tf_op jit(solution)/shard_map/ppermute | solution.py:648
  485.1 5.9 %unproject.7 = (f32[512,1024]{1,0:T(8,128)}, f32[1,1024]{1,0:T(1,128)}) custom-call(s32[1]{0:T(128)S(6)} %rem.79.blk_ref, bf16[2048,768]{1,0:T(8,128)(2,1)} %get-tuple-element.95.g_ref, bf16[1024,768]{1,0:T(8,128)(2,1)} %all-gather.2.cloned.1.call-done.w_ref, bf16[512,1024]{1,0:T(8,128)(2,1)} %x_ref.5, f32[1,1024]{1,0:T(1,128)} %bitcast.146, ...), custom_call_target="tpu_custom_call" | custom-call | flops 805306368 | bytes 5242880 | tf_op jit(solution)/shard_map/unproject/pallas_call | solution.py:132
  496.6 5.6 %all-to-all-done.3 = f32[32,2,32]{2,1,0:T(2,128)S(1)} async-done(((f32[32,2,32]{2,1,0:T(2,128)}), f32[32,2,32]{2,1,0:T(2,128)S(1)}, u32[]{:S(2)}, u32[]{:S(2)}) %all-to-all-start.3) | async-done | bytes 8224 | tf_op jit(solution)/shard_map/all_to_all | solution.py:780
  (230 shorter events, 134.8 us)
Async XLA Ops:
  12.7 125.1 %all-gather.2.cloned.1.call-start = ((), (), s32[]{:S(2)}) async-start(), calls=%async_computation.8 | async-start | bytes 1769472 | tf_op jit(solution)/shard_map/all_gather | solution.py:665
  21.1 39.3 %collective-permute-start = (bf16[512,1024]{1,0:T(8,128)(2,1)S(1)}, bf16[512,1024]{1,0:T(8,128)(2,1)S(1)}, u32[]{:S(2)}, u32[]{:S(2)}) collective-permute-start(bf16[512,1024]{1,0:T(8,128)(2,1)S(1)} %copy-done.4), channel_id=1, source_target_pairs={{0,1},{1,2},{2,3},{3,0},{4,5},{5,6},{6,7},{7,4},{8,9},{9,10},{10,1... | collective-permute-start | bytes 3145736 | tf_op jit(solution)/shard_map/ppermute | solution.py:648
  38.1 36.0 %collective-permute-start.8 = (bf16[1184,256]{1,0:T(8,128)(2,1)}, bf16[1184,256]{1,0:T(8,128)(2,1)}, u32[]{:S(2)}, u32[]{:S(2)}) collective-permute-start(bf16[1184,256]{1,0:T(8,128)(2,1)} %collective-permute-done.6.rest_4_), channel_id=1, source_target_pairs={{0,16},{8,24},{16,0},{24,8},{1,17},{9,25},{17,1},{25,9},{2,18},{10... | collective-permute-start | bytes 1818632 | tf_op jit(solution)/shard_map/ppermute | solution.py:649
  38.6 35.0 %collective-permute-start.10 = (bf16[1184,256]{1,0:T(8,128)(2,1)}, bf16[1184,256]{1,0:T(8,128)(2,1)}, u32[]{:S(2)}, u32[]{:S(2)}) collective-permute-start(bf16[1184,256]{1,0:T(8,128)(2,1)} %collective-permute-done.6.rest_4_), channel_id=1, source_target_pairs={{0,1},{1,2},{2,3},{3,0},{4,5},{5,6},{6,7},{7,4},{8,9},{9,10},{10,1... | collective-permute-start | bytes 1818632 | tf_op jit(solution)/shard_map/ppermute | solution.py:648
  38.6 35.5 %collective-permute-start.5 = (bf16[1184,256]{1,0:T(8,128)(2,1)S(1)}, bf16[1184,256]{1,0:T(8,128)(2,1)}, u32[]{:S(2)}, u32[]{:S(2)}) collective-permute-start(bf16[1184,256]{1,0:T(8,128)(2,1)S(1)} %collective-permute-done.3.rest_1_), channel_id=1, source_target_pairs={{0,16},{8,24},{16,0},{24,8},{1,17},{9,25},{17,1},{25,9},{2,18},{10... | collective-permute-start | bytes 1818632 | tf_op jit(solution)/shard_map/ppermute | solution.py:649
  45.8 32.8 %collective-permute-start.7 = (bf16[1184,256]{1,0:T(8,128)(2,1)}, bf16[1184,256]{1,0:T(8,128)(2,1)S(1)}, u32[]{:S(2)}, u32[]{:S(2)}) collective-permute-start(bf16[1184,256]{1,0:T(8,128)(2,1)} %collective-permute-done.6.rest_4_), channel_id=1, source_target_pairs={{0,8},{8,0},{16,24},{24,16},{1,9},{9,1},{17,25},{25,17},{2,10},{10... | collective-permute-start | bytes 1818632 | tf_op jit(solution)/shard_map/ppermute | solution.py:649
  60.4 51.9 %collective-permute-start.1 = (bf16[512,1024]{1,0:T(8,128)(2,1)S(1)}, bf16[512,1024]{1,0:T(8,128)(2,1)S(1)}, u32[]{:S(2)}, u32[]{:S(2)}) collective-permute-start(bf16[512,1024]{1,0:T(8,128)(2,1)S(1)} %collective-permute-done.x_ref), channel_id=1, source_target_pairs={{0,1},{1,2},{2,3},{3,0},{4,5},{5,6},{6,7},{7,4},{8,9},{9,10},{10,1... | collective-permute-start | bytes 3145736 | tf_op jit(solution)/shard_map/ppermute | solution.py:648
  73.5 35.1 %collective-permute-start.11 = (bf16[1184,256]{1,0:T(8,128)(2,1)}, bf16[1184,256]{1,0:T(8,128)(2,1)S(1)}, u32[]{:S(2)}, u32[]{:S(2)}) collective-permute-start(bf16[1184,256]{1,0:T(8,128)(2,1)} %collective-permute-done.10.rest_8_), channel_id=1, source_target_pairs={{0,8},{8,0},{16,24},{24,16},{1,9},{9,1},{17,25},{25,17},{2,10},{10... | collective-permute-start | bytes 1818632 | tf_op jit(solution)/shard_map/ppermute | solution.py:649
  74.1 33.5 %collective-permute-start.14 = (bf16[1184,256]{1,0:T(8,128)(2,1)}, bf16[1184,256]{1,0:T(8,128)(2,1)}, u32[]{:S(2)}, u32[]{:S(2)}) collective-permute-start(bf16[1184,256]{1,0:T(8,128)(2,1)} %collective-permute-done.10.rest_8_), channel_id=1, source_target_pairs={{0,1},{1,2},{2,3},{3,0},{4,5},{5,6},{6,7},{7,4},{8,9},{9,10},{10,1... | collective-permute-start | bytes 1818632 | tf_op jit(solution)/shard_map/ppermute | solution.py:648
  74.1 34.1 %collective-permute-start.9 = (bf16[1184,256]{1,0:T(8,128)(2,1)}, bf16[1184,256]{1,0:T(8,128)(2,1)S(1)}, u32[]{:S(2)}, u32[]{:S(2)}) collective-permute-start(bf16[1184,256]{1,0:T(8,128)(2,1)} %collective-permute-done.8.rest_6_), channel_id=1, source_target_pairs={{0,8},{8,0},{16,24},{24,16},{1,9},{9,1},{17,25},{25,17},{2,10},{10... | collective-permute-start | bytes 1818632 | tf_op jit(solution)/shard_map/ppermute | solution.py:649
  78.6 34.7 %collective-permute-start.12 = (bf16[1184,256]{1,0:T(8,128)(2,1)}, bf16[1184,256]{1,0:T(8,128)(2,1)S(1)}, u32[]{:S(2)}, u32[]{:S(2)}) collective-permute-start(bf16[1184,256]{1,0:T(8,128)(2,1)} %collective-permute-done.10.rest_8_), channel_id=1, source_target_pairs={{0,16},{8,24},{16,0},{24,8},{1,17},{9,25},{17,1},{25,9},{2,18},{10... | collective-permute-start | bytes 1818632 | tf_op jit(solution)/shard_map/ppermute | solution.py:649
  107.6 73.2 %collective-permute-start.15 = (bf16[1184,256]{1,0:T(8,128)(2,1)}, bf16[1184,256]{1,0:T(8,128)(2,1)}, u32[]{:S(2)}, u32[]{:S(2)}) collective-permute-start(bf16[1184,256]{1,0:T(8,128)(2,1)} %collective-permute-done.14.rest_12_), channel_id=1, source_target_pairs={{0,8},{8,0},{16,24},{24,16},{1,9},{9,1},{17,25},{25,17},{2,10},{10... | collective-permute-start | bytes 1818632 | tf_op jit(solution)/shard_map/ppermute | solution.py:649
  112.3 37.6 %collective-permute-start.2 = (bf16[512,1024]{1,0:T(8,128)(2,1)S(1)}, bf16[512,1024]{1,0:T(8,128)(2,1)S(1)}, u32[]{:S(2)}, u32[]{:S(2)}) collective-permute-start(bf16[512,1024]{1,0:T(8,128)(2,1)S(1)} %collective-permute-done.1.x_ref), channel_id=1, source_target_pairs={{0,1},{1,2},{2,3},{3,0},{4,5},{5,6},{6,7},{7,4},{8,9},{9,10},{10,1... | collective-permute-start | bytes 3145736 | tf_op jit(solution)/shard_map/ppermute | solution.py:648
  125.1 58.7 %collective-permute-start.17 = (bf16[1184,256]{1,0:T(8,128)(2,1)}, bf16[1184,256]{1,0:T(8,128)(2,1)}, u32[]{:S(2)}, u32[]{:S(2)}) collective-permute-start(bf16[1184,256]{1,0:T(8,128)(2,1)} %collective-permute-done.16.rest_14_), channel_id=1, source_target_pairs={{0,8},{8,0},{16,24},{24,16},{1,9},{9,1},{17,25},{25,17},{2,10},{10... | collective-permute-start | bytes 1818632 | tf_op jit(solution)/shard_map/ppermute | solution.py:649
  251.3 181.6 %collective-permute-start.21 = (bf16[512,1024]{1,0:T(8,128)(2,1)}, bf16[512,1024]{1,0:T(8,128)(2,1)}, u32[]{:S(2)}, u32[]{:S(2)}) collective-permute-start(bf16[512,1024]{1,0:T(8,128)(2,1)} %get-tuple-element.90), channel_id=1, source_target_pairs={{0,4},{4,0},{1,5},{5,1},{2,6},{6,2},{3,7},{7,3},{8,12},{12,8},{9,1... | collective-permute-start | bytes 3145736 | tf_op jit(solution)/shard_map/ppermute | solution.py:647
  251.5 34.9 %collective-permute-start.22 = (bf16[512,1024]{1,0:T(8,128)(2,1)S(1)}, bf16[512,1024]{1,0:T(8,128)(2,1)S(1)}, u32[]{:S(2)}, u32[]{:S(2)}) collective-permute-start(bf16[512,1024]{1,0:T(8,128)(2,1)S(1)} %copy-done.38), channel_id=1, source_target_pairs={{0,4},{4,0},{1,5},{5,1},{2,6},{6,2},{3,7},{7,3},{8,12},{12,8},{9,1... | collective-permute-start | bytes 3145736 | tf_op jit(solution)/shard_map/ppermute | solution.py:647
  267.6 40.1 %collective-permute-start.35 = (bf16[1056,256]{1,0:T(8,128)(2,1)}, bf16[1056,256]{1,0:T(8,128)(2,1)}, u32[]{:S(2)}, u32[]{:S(2)}) collective-permute-start(bf16[1056,256]{1,0:T(8,128)(2,1)} %get-tuple-element.125), channel_id=1, source_target_pairs={{0,8},{8,0},{16,24},{24,16},{1,9},{9,1},{17,25},{25,17},{2,10},{10... | collective-permute-start | bytes 1622024 | tf_op jit(solution)/shard_map/ppermute | solution.py:649
  268.1 31.8 %collective-permute-start.33 = (bf16[1056,256]{1,0:T(8,128)(2,1)}, bf16[1056,256]{1,0:T(8,128)(2,1)S(1)}, u32[]{:S(2)}, u32[]{:S(2)}) collective-permute-start(bf16[1056,256]{1,0:T(8,128)(2,1)} %get-tuple-element.123), channel_id=1, source_target_pairs={{0,16},{8,24},{16,0},{24,8},{1,17},{9,25},{17,1},{25,9},{2,18},{10... | collective-permute-start | bytes 1622024 | tf_op jit(solution)/shard_map/ppermute | solution.py:649
  283.3 107.2 %collective-permute-start.32 = (bf16[1056,256]{1,0:T(8,128)(2,1)}, bf16[1056,256]{1,0:T(8,128)(2,1)}, u32[]{:S(2)}, u32[]{:S(2)}) collective-permute-start(bf16[1056,256]{1,0:T(8,128)(2,1)} %get-tuple-element.121), channel_id=1, source_target_pairs={{0,16},{8,24},{16,0},{24,8},{1,17},{9,25},{17,1},{25,9},{2,18},{10... | collective-permute-start | bytes 1622024 | tf_op jit(solution)/shard_map/ppermute | solution.py:649
  296.2 31.7 %all-to-all-start.2 = ((bf16[512,4,256]{2,0,1:T(8,128)(2,1)}), bf16[512,4,256]{2,0,1:T(8,128)(2,1)S(1)}, u32[]{:S(2)}, u32[]{:S(2)}) async-start(bf16[512,4,256]{2,0,1:T(8,128)(2,1)} %bitcast.118), calls=%async_computation.2 | async-start | bytes 2097152 | tf_op jit(solution)/shard_map/all_to_all | solution.py:716
  299.9 120.7 %reduce-scatter.6.cloned.1.call-start = ((), (), s32[]{:S(2)}) async-start(), calls=%async_computation.10 | async-start | bytes 2359296 | tf_op jit(solution)/shard_map/reduce_scatter | solution.py:752
  299.9 87.0 %collective-permute-start.27 = (bf16[1056,256]{1,0:T(8,128)(2,1)}, bf16[1056,256]{1,0:T(8,128)(2,1)}, u32[]{:S(2)}, u32[]{:S(2)}) collective-permute-start(bf16[1056,256]{1,0:T(8,128)(2,1)} %get-tuple-element.115), channel_id=1, source_target_pairs={{0,16},{8,24},{16,0},{24,8},{1,17},{9,25},{17,1},{25,9},{2,18},{10... | collective-permute-start | bytes 1622024 | tf_op jit(solution)/shard_map/ppermute | solution.py:649
  307.7 167.0 %reduce-scatter.8.cloned.1.call-start = ((), (), s32[]{:S(2)}) async-start(), calls=%async_computation.11 | async-start | bytes 327680 | tf_op jit(solution)/shard_map/reduce_scatter | solution.py:751
  308.7 83.2 %collective-permute-start.34 = (bf16[1056,256]{1,0:T(8,128)(2,1)S(1)}, bf16[1056,256]{1,0:T(8,128)(2,1)S(1)}, u32[]{:S(2)}, u32[]{:S(2)}) collective-permute-start(bf16[1056,256]{1,0:T(8,128)(2,1)S(1)} %copy-done.23), channel_id=1, source_target_pairs={{0,8},{8,0},{16,24},{24,16},{1,9},{9,1},{17,25},{25,17},{2,10},{10... | collective-permute-start | bytes 1622024 | tf_op jit(solution)/shard_map/ppermute | solution.py:649
  326.2 66.4 %collective-permute-start.38 = (bf16[1056,256]{1,0:T(8,128)(2,1)S(1)}, bf16[1056,256]{1,0:T(8,128)(2,1)S(1)}, u32[]{:S(2)}, u32[]{:S(2)}) collective-permute-start(bf16[1056,256]{1,0:T(8,128)(2,1)S(1)} %add_convert_fusion.4), channel_id=1, source_target_pairs={{0,1},{1,2},{2,3},{3,0},{4,5},{5,6},{6,7},{7,4},{8,9},{9,10},{10,1... | collective-permute-start | bytes 1622024 | tf_op jit(solution)/shard_map/ppermute | solution.py:648
  390.6 37.0 %collective-permute-start.29 = (bf16[1056,256]{1,0:T(8,128)(2,1)}, bf16[1056,256]{1,0:T(8,128)(2,1)}, u32[]{:S(2)}, u32[]{:S(2)}) collective-permute-start(bf16[1056,256]{1,0:T(8,128)(2,1)} %get-tuple-element.117), channel_id=1, source_target_pairs={{0,8},{8,0},{16,24},{24,16},{1,9},{9,1},{17,25},{25,17},{2,10},{10... | collective-permute-start | bytes 1622024 | tf_op jit(solution)/shard_map/ppermute | solution.py:649
  391.9 36.8 %collective-permute-start.31 = (bf16[1056,256]{1,0:T(8,128)(2,1)}, bf16[1056,256]{1,0:T(8,128)(2,1)}, u32[]{:S(2)}, u32[]{:S(2)}) collective-permute-start(bf16[1056,256]{1,0:T(8,128)(2,1)} %add_convert_fusion.11), channel_id=1, source_target_pairs={{0,16},{8,24},{16,0},{24,8},{1,17},{9,25},{17,1},{25,9},{2,18},{10... | collective-permute-start | bytes 1622024 | tf_op jit(solution)/shard_map/ppermute | solution.py:649
  394.8 34.9 %collective-permute-start.39 = (bf16[1056,256]{1,0:T(8,128)(2,1)}, bf16[1056,256]{1,0:T(8,128)(2,1)}, u32[]{:S(2)}, u32[]{:S(2)}) collective-permute-start(bf16[1056,256]{1,0:T(8,128)(2,1)} %add_convert_fusion.3), channel_id=1, source_target_pairs={{0,1},{1,2},{2,3},{3,0},{4,5},{5,6},{6,7},{7,4},{8,9},{9,10},{10,1... | collective-permute-start | bytes 1622024 | tf_op jit(solution)/shard_map/ppermute | solution.py:648
  420.6 32.9 %collective-permute-start.24 = (bf16[512,1024]{1,0:T(8,128)(2,1)}, bf16[512,1024]{1,0:T(8,128)(2,1)}, u32[]{:S(2)}, u32[]{:S(2)}) collective-permute-start(bf16[512,1024]{1,0:T(8,128)(2,1)} %get-tuple-element.97), channel_id=1, source_target_pairs={{0,1},{1,2},{2,3},{3,0},{4,5},{5,6},{6,7},{7,4},{8,9},{9,10},{10,1... | collective-permute-start | bytes 3145736 | tf_op jit(solution)/shard_map/ppermute | solution.py:648
  420.6 74.3 %reduce-scatter.4.cloned.1.call-start = ((), (), s32[]{:S(2)}) async-start(), calls=%async_computation.9 | async-start | bytes 1769472 | tf_op jit(solution)/shard_map/reduce_scatter | solution.py:771
  427.6 30.5 %collective-permute-start.26 = (bf16[1056,256]{1,0:T(8,128)(2,1)}, bf16[1056,256]{1,0:T(8,128)(2,1)S(1)}, u32[]{:S(2)}, u32[]{:S(2)}) collective-permute-start(bf16[1056,256]{1,0:T(8,128)(2,1)} %get-tuple-element.113), channel_id=1, source_target_pairs={{0,16},{8,24},{16,0},{24,8},{1,17},{9,25},{17,1},{25,9},{2,18},{10... | collective-permute-start | bytes 1622024 | tf_op jit(solution)/shard_map/ppermute | solution.py:649
  431.7 33.3 %collective-permute-start.40 = (bf16[1056,256]{1,0:T(8,128)(2,1)S(1)}, bf16[1056,256]{1,0:T(8,128)(2,1)S(1)}, u32[]{:S(2)}, u32[]{:S(2)}) collective-permute-start(bf16[1056,256]{1,0:T(8,128)(2,1)S(1)} %add_convert_fusion.2), channel_id=1, source_target_pairs={{0,1},{1,2},{2,3},{3,0},{4,5},{5,6},{6,7},{7,4},{8,9},{9,10},{10,1... | collective-permute-start | bytes 1622024 | tf_op jit(solution)/shard_map/ppermute | solution.py:648
  (57 other events, 755.3 us)
Sparse Core Ops, SparseCore 0:
  23.6 29.5 all-gather.1
  307.8 41.1 reduce-scatter.5
  420.7 22.7 reduce-scatter.7
  446.7 37.5 reduce-scatter.3
